TPU v7x, 128 devices: a whole 4x4x4 slice. The times are simulated.
128 devices in a mesh: grp: 4 (over z), blk: 32 (over x, y, core).
Axes of the slice: x: 4, y: 4, z: 4, core: 2. Of those that a mesh axis runs over, the one named last changes fastest.
Arguments:
- barrier_scale: float32 [384, 1536], P(('grp', 'blk')), may hold values from 0.1 to 10
- regularizer: float32 [384, 768], P(('grp', 'blk')), may hold values from 0.5 to 1.5
- availability: float32 [384, 768], P(('grp', 'blk')), may hold values from 0.2 to 1
- block_rhs: float32 [384, 768], P(('grp', 'blk')), may hold values from -6 to 6
- primal: float32 [384, 1536], P(('grp', 'blk')), may hold values from -6 to 6
- link_mask: int32 [384, 128], P(('grp', 'blk')), may hold values 0 or 1
- counts: int32 [128], P(('grp', 'blk')), may hold values from 1 to 3, as said below
- constraints: bfloat16 [768, 1536], replicated, may hold values from -0.15625 to 0.15625
- border: float32 [768, 768], replicated, may hold values from -0.21875 to 0.21875
- link_out: float32 [128, 1536], replicated, may hold values from -0.15625 to 0.15625
- link_in: float32 [768, 128], replicated, may hold values from -0.5 to 0.5
- first_diag: float32 [768], replicated, may hold values from 5.12 to 51.2
- first_rhs: float32 [768], replicated, may hold values from -320 to 320
Outputs:
- block_step: float32 [384, 768], P(('grp', 'blk'))
- first_step: float32 [768], replicated
Inputs may be any that keep to these rules, and one draw needn't show every extreme that they name: Device d holds its first counts[d] slots; slots from counts[d] on are empty and ignored. Devices 2k and 2k+1 together hold exactly 4 hours; some device holds exactly 3 and some exactly 1.
All inputs are finite; a program needn't handle non-finite values. No bound on the sum of `link_mask` on one device may be relied on, other than what follows from the above.
Results may differ from a plain program's by a relative error of at most 0.0013.
Values sent between devices are 32-bit elements; how exact they have to be, the bound alone decides.
No kernel may reach another device: no remote copies, remote signals or barrier semaphores. Data moves between devices by JAX's collectives and lax.ppermute only.
A program may use at most 128 MiB of HBM per device.

v0:
```python
import math

import jax
import jax.numpy as jnp
from jax import lax
from jax.sharding import Mesh
from jax.sharding import PartitionSpec as P

BPD = 2
GRP_BLK = ("grp", "blk_0", "blk_1", "blk_2")
BLK = ("blk_0", "blk_1", "blk_2")


HIGHEST_PRECISION = lax.Precision.HIGHEST


def passed_along(value, axis, steps):
    count = lax.axis_size(axis)
    initial, last = (max(0, -steps), min(count, count - steps))
    return lax.ppermute(value, axis, [(source, source + steps) for source in range(initial, last)])


def filled_with(array, identity):
    return jnp.broadcast_to(jnp.asarray(identity, array.dtype), array.shape)


def prefix_by_axis(array, axes, combine, identity):
    before = start = filled_with(array, identity)
    subtotal = array
    for axis in reversed(axes):
        length, here = (lax.axis_size(axis), lax.axis_index(axis))
        pieces = lax.all_gather(subtotal, axis)
        inside, subtotal = (start, start)
        for k in range(length):
            passed = k < here
            subtotal = combine(subtotal, pieces[k])
            inside = jnp.where(passed, subtotal, inside)
        before = combine(inside, before)
    return before


def swapped(value, axis, bit):
    mask = 2**bit
    pairs = [(source, source ^ mask) for source in range(lax.axis_size(axis))]
    return lax.ppermute(value, axis, pairs)


def in_blocks(array, dim, length):
    before, after = (array.shape[:dim], array.shape[dim + 1 :])
    return jnp.moveaxis(array.reshape(*before, length, -1, *after), dim, 0)


def summed_on_arrival(array, axis, dim):
    pieces = in_blocks(array, dim, lax.axis_size(axis))
    arrived = lax.all_to_all(pieces, axis, split_axis=0, concat_axis=0, tiled=True)
    return arrived.sum(axis=0)


def side_by_side(arrays, axis, dim, along):
    widths = [math.prod(a.shape[along:]) for a in arrays]
    both = jnp.concatenate(
        [a.reshape(*a.shape[:along], w) for a, w in zip(arrays, widths)], axis=along
    )
    out = summed_on_arrival(both, axis, dim)
    pieces = jnp.split(out, [sum(widths[:k]) for k in range(1, len(widths))], axis=along)
    return tuple((b.reshape(*out.shape[:along], *a.shape[along:]) for a, b in zip(arrays, pieces)))


def sent_to_all(array, axis):
    length = lax.axis_size(axis)
    return lax.all_to_all(
        jnp.broadcast_to(array[None], (length, *array.shape)), axis, 0, 0, tiled=True
    )


def of_everyone(array, axis):
    return sent_to_all(array, axis).sum(axis=0)


def in_one(arrays, axis):
    ends = [0]
    for a in arrays:
        ends.append(ends[-1] + a.size)
    subtotal = of_everyone(jnp.concatenate([a.ravel() for a in arrays]), axis)
    return tuple((subtotal[b:e].reshape(a.shape) for a, b, e in zip(arrays, ends, ends[1:])))


def in_order(pieces, dim):
    pieces = jnp.moveaxis(pieces, 0, dim)
    lengths = pieces.shape
    return pieces.reshape(*lengths[:dim], lengths[dim] * lengths[dim + 1], *lengths[dim + 2 :])


def gather_directly(array, axis, dim):
    return in_order(sent_to_all(array, axis), dim)


def in_one_piece(arrays, axis, dim, along):
    widths = [math.prod(a.shape[along:]) for a in arrays]
    both = jnp.concatenate(
        [a.reshape(*a.shape[:along], w) for a, w in zip(arrays, widths)], axis=along
    )
    out = gather_directly(both, axis, dim)
    pieces = jnp.split(out, [sum(widths[:k]) for k in range(1, len(widths))], axis=along)
    return tuple((b.reshape(*out.shape[:along], *a.shape[along:]) for a, b in zip(arrays, pieces)))


def factor_block(scale_row, diag_row, constraints):
    scaled = (constraints.astype(jnp.float32) * scale_row[None, :]).astype(jnp.bfloat16)
    kkt = lax.dot_general(
        scaled, constraints, (((1,), (1,)), ((), ())), preferred_element_type=jnp.float32
    )
    kkt = kkt + jnp.diag(diag_row)
    return jnp.linalg.cholesky(kkt)


def schur_terms(barrier_scale, regularizer, availability, corrected, weights, constraints, border):
    first_width = border.shape[1]

    def accumulate(partial_sums, block_items):
        schur_part, first_grad = partial_sums
        scale_row, diag_row, avail_row, corrected_row, weight = block_items
        lower_factor = factor_block(scale_row, diag_row, constraints)
        solved = jax.scipy.linalg.solve_triangular(
            lower_factor, avail_row[:, None] * border, lower=True
        )
        reduced = jax.scipy.linalg.solve_triangular(lower_factor, corrected_row, lower=True)
        gram_term = lax.dot_general(
            solved,
            solved,
            (((0,), (0,)), ((), ())),
            precision=HIGHEST_PRECISION,
            preferred_element_type=jnp.float32,
        )
        inner_term = lax.dot_general(
            solved,
            reduced,
            (((0,), (0,)), ((), ())),
            precision=HIGHEST_PRECISION,
            preferred_element_type=jnp.float32,
        )
        return ((schur_part + weight * gram_term, first_grad + weight * inner_term), lower_factor)

    initial = (
        jnp.zeros((first_width, first_width), jnp.float32),
        jnp.zeros((first_width,), jnp.float32),
    )
    (schur_part, first_grad), lowers = lax.scan(
        accumulate, initial, (barrier_scale, regularizer, availability, corrected, weights)
    )
    return (schur_part, first_grad, lowers)


def back_solve(lowers, availability, corrected, coupled):

    def single(block_items):
        lower_factor, avail_row, corrected_row = block_items
        residual = corrected_row - avail_row * coupled
        halfway = jax.scipy.linalg.solve_triangular(lower_factor, residual, lower=True)
        return jax.scipy.linalg.solve_triangular(lower_factor, halfway, lower=True, trans=1)

    return lax.map(single, (lowers, availability, corrected))


def select_rows(chooser, source):
    return jnp.dot(chooser, source, precision=HIGHEST_PRECISION, preferred_element_type=jnp.float32)


def on_device(
    barrier_scale,
    regularizer,
    availability,
    block_rhs,
    primal,
    link_mask,
    counts,
    constraints,
    border,
    link_out,
    link_in,
    first_diag,
    first_rhs,
):
    capacity = barrier_scale.shape[0]
    own_count = counts[0]
    slot_ids = jnp.arange(capacity, dtype=jnp.int32)
    live_slots = slot_ids < own_count
    link_state = lax.dot_general(
        primal,
        link_out,
        (((1,), (1,)), ((), ())),
        precision=HIGHEST_PRECISION,
        preferred_element_type=jnp.float32,
    )
    last_state = lax.dynamic_index_in_dim(link_state, own_count - 1, 0, keepdims=False)
    incoming = passed_along(last_state, GRP_BLK, 1)
    previous = jnp.concatenate([incoming[None, :], link_state[:-1]], axis=0)
    linked = link_mask.astype(jnp.float32) * previous
    corrected = block_rhs + lax.dot_general(
        linked,
        link_in,
        (((1,), (1,)), ((), ())),
        precision=HIGHEST_PRECISION,
        preferred_element_type=jnp.float32,
    )
    offsets = prefix_by_axis(
        counts, GRP_BLK, lambda earlier, later: earlier + later, jnp.zeros((1,), jnp.int32)
    )
    offset_rows = offsets[0]
    block_tags = jnp.where(live_slots, offset_rows + slot_ids, -1).astype(jnp.float32)
    position = lax.axis_index(GRP_BLK)
    targets = (position * BPD + jnp.arange(BPD, dtype=jnp.int32)).astype(jnp.float32)
    partner = swapped((block_tags, barrier_scale, regularizer, availability, corrected), GRP_BLK, 0)
    pair_tags = jnp.concatenate([block_tags, partner[0]], axis=0)
    chooser = (pair_tags[None, :] == targets[:, None]).astype(jnp.float32)
    work_scale = select_rows(chooser, jnp.concatenate([barrier_scale, partner[1]], axis=0))
    work_diag = select_rows(chooser, jnp.concatenate([regularizer, partner[2]], axis=0))
    work_avail = select_rows(chooser, jnp.concatenate([availability, partner[3]], axis=0))
    work_corrected = select_rows(chooser, jnp.concatenate([corrected, partner[4]], axis=0))
    weights = jnp.ones((BPD,), jnp.float32)
    schur_part, first_grad, lowers = schur_terms(
        work_scale, work_diag, work_avail, work_corrected, weights, constraints, border
    )
    row_share = side_by_side((schur_part, first_grad), BLK, 0, 1)
    row_share = in_one((row_share[0], row_share[1]), "grp")
    schur_total, grad_total = in_one_piece((row_share[0], row_share[1]), BLK, 0, 1)
    schur_matrix = schur_total + jnp.diag(first_diag)
    schur_factor = jnp.linalg.cholesky(schur_matrix)
    first_step = jax.scipy.linalg.cho_solve((schur_factor, True), grad_total - first_rhs)
    coupled = jnp.dot(
        border, first_step, precision=HIGHEST_PRECISION, preferred_element_type=jnp.float32
    )
    solutions = back_solve(lowers, work_avail, work_corrected, coupled)
    returned = swapped(solutions, GRP_BLK, 0)
    partner_targets = (
        jnp.bitwise_xor(position, 1) * BPD + jnp.arange(BPD, dtype=jnp.int32)
    ).astype(jnp.float32)
    all_targets = jnp.concatenate([targets, partner_targets], axis=0)
    all_solutions = jnp.concatenate([solutions, returned], axis=0)
    picker = (block_tags[:, None] == all_targets[None, :]).astype(jnp.float32)
    block_step = select_rows(picker, all_solutions)
    return (block_step, first_step)


def solution(mesh):
    split = Mesh(
        mesh.devices.reshape(mesh.shape["grp"], 4, 4, 2), ("grp", "blk_0", "blk_1", "blk_2")
    )
    placed = (
        P(GRP_BLK, None),
        P(GRP_BLK, None),
        P(GRP_BLK, None),
        P(GRP_BLK, None),
        P(GRP_BLK, None),
        P(GRP_BLK, None),
        P(GRP_BLK),
        P(),
        P(),
        P(),
        P(),
        P(),
        P(),
    )
    return jax.shard_map(
        on_device, mesh=split, in_specs=placed, out_specs=(P(GRP_BLK, None), P()), check_vma=False
    )
```

profile of v0, /device:TPU:1, one launch (start us, length us, event | category | flops | bytes accessed | tf_op | source)
XLA Modules:
  0.0 1147.4 jit_solution(15053855568798701513)
XLA Ops:
  9.5 7.1 all-reduce.2
  21.1 6.9 all-reduce.3
  32.2 7.7 all-reduce.4
  49.9 6.5 collective-permute-start
  65.8 533.9 %while.42 = (s32[]{:T(128)}, f32[768,768]{1,0:T(8,128)}, f32[768]{0:T(1024)}, f32[2,768,768]{1,2,0:T(8,128)}, bf16[768,1536]{1,0:T(8,128)(2,1)}, /*index=5*/f32[...) while((s32[]{:T(128)}, f32[768,768]{1,0:T(8,128)}, ...), condition=%wide.region_13.16_spmd.clone, body=%wide.region_0.15_spmd.clone.sunk | while | flops 11703703552 | bytes 84802688 | solution.py:148
  66.4 4.4 select_add_fusion.7
  76.3 11.7 %cholesky.1234 = f32[128,128]{1,0:T(8,128)S(1)} custom-call(f32[128,128]{1,0:T(8,128)S(1)} %cholesky.1233), custom_call_target="Cholesky" | custom-call | tf_op jit(solution)/shard_map/while/body/eval_jaxpr/jit(cholesky)/cholesky | solution.py:114
  88.0 9.8 custom-call.114
  100.6 11.7 %cholesky.1237 = f32[128,128]{1,0:T(8,128)S(1)} custom-call(f32[128,128]{1,0:T(8,128)S(1)} %cholesky.1236), custom_call_target="Cholesky" | custom-call | tf_op jit(solution)/shard_map/while/body/eval_jaxpr/jit(cholesky)/cholesky | solution.py:114
  115.5 10.8 custom-call.115
  128.7 11.7 %cholesky.1239 = f32[128,128]{1,0:T(8,128)S(1)} custom-call(f32[128,128]{1,0:T(8,128)S(1)} %cholesky.1238), custom_call_target="Cholesky" | custom-call | tf_op jit(solution)/shard_map/while/body/eval_jaxpr/jit(cholesky)/cholesky | solution.py:114
  141.9 9.8 custom-call.116
  154.2 11.9 %cholesky.1241 = f32[128,128]{1,0:T(8,128)S(1)} custom-call(f32[128,128]{1,0:T(8,128)S(1)} %cholesky.1240), custom_call_target="Cholesky" | custom-call | tf_op jit(solution)/shard_map/while/body/eval_jaxpr/jit(cholesky)/cholesky | solution.py:114
  167.6 9.8 custom-call.117
  179.7 11.7 %cholesky.1243 = f32[128,128]{1,0:T(8,128)S(1)} custom-call(f32[128,128]{1,0:T(8,128)S(1)} %cholesky.1242), custom_call_target="Cholesky" | custom-call | tf_op jit(solution)/shard_map/while/body/eval_jaxpr/jit(cholesky)/cholesky | solution.py:114
  192.8 9.8 custom-call.118
  204.9 11.7 %cholesky.1244 = f32[128,128]{1,0:T(8,128)S(1)} custom-call(f32[128,128]{1,0:T(8,128)S(1)} %convolution_subtract_fusion.27), custom_call_target="Cholesky" | custom-call | tf_op jit(solution)/shard_map/while/body/eval_jaxpr/jit(cholesky)/cholesky | solution.py:114
  221.3 18.5 %while.45 = (s32[]{:T(128)}, f32[768,768]{0,1:T(8,128)}, s32[6,2]{0,1:T(2,128)S(1)}, f32[6,128,128]{2,1,0:T(8,128)S(1)}, s32[]{:T(128)}) while((s32[]{:T(128)}, f32[768,768]{0,1:T(8,128)}, s32[6,2]{0,1:T(2,128)S(1)}, f32[6,128,128]{2,1,0:T(8,128)S(1)}, s32[]{:T(128)}) %tuple.228), condition=%wide.while_cond.1, body=%wide.while_body.1.sunk | while | flops 2 | bytes 393321 | solution.py:124
  239.8 59.1 %custom-call.120 = f32[6,128,128]{1,2,0:T(8,128)S(1)} custom-call(f32[6,128,128]{2,1,0:T(8,128)S(1)} %get-tuple-element.702), custom_call_target="InvertDiagBlocksLowerTriangular" | custom-call | tf_op jit(solution)/shard_map/while/body/eval_jaxpr/jit(_solve_triangular)/triangular_solve | solution.py:124
  321.3 7.8 select_add_fusion.8
  331.6 4.4 select_add_fusion.7
  341.4 11.7 %cholesky.1234 = f32[128,128]{1,0:T(8,128)S(1)} custom-call(f32[128,128]{1,0:T(8,128)S(1)} %cholesky.1233), custom_call_target="Cholesky" | custom-call | tf_op jit(solution)/shard_map/while/body/eval_jaxpr/jit(cholesky)/cholesky | solution.py:114
  353.2 9.8 custom-call.114
  365.8 11.7 %cholesky.1237 = f32[128,128]{1,0:T(8,128)S(1)} custom-call(f32[128,128]{1,0:T(8,128)S(1)} %cholesky.1236), custom_call_target="Cholesky" | custom-call | tf_op jit(solution)/shard_map/while/body/eval_jaxpr/jit(cholesky)/cholesky | solution.py:114
  380.7 10.8 custom-call.115
  393.9 11.7 %cholesky.1239 = f32[128,128]{1,0:T(8,128)S(1)} custom-call(f32[128,128]{1,0:T(8,128)S(1)} %cholesky.1238), custom_call_target="Cholesky" | custom-call | tf_op jit(solution)/shard_map/while/body/eval_jaxpr/jit(cholesky)/cholesky | solution.py:114
  407.1 9.8 custom-call.116
  419.4 11.9 %cholesky.1241 = f32[128,128]{1,0:T(8,128)S(1)} custom-call(f32[128,128]{1,0:T(8,128)S(1)} %cholesky.1240), custom_call_target="Cholesky" | custom-call | tf_op jit(solution)/shard_map/while/body/eval_jaxpr/jit(cholesky)/cholesky | solution.py:114
  432.8 9.8 custom-call.117
  444.8 11.7 %cholesky.1243 = f32[128,128]{1,0:T(8,128)S(1)} custom-call(f32[128,128]{1,0:T(8,128)S(1)} %cholesky.1242), custom_call_target="Cholesky" | custom-call | tf_op jit(solution)/shard_map/while/body/eval_jaxpr/jit(cholesky)/cholesky | solution.py:114
  458.0 9.8 custom-call.118
  470.1 11.7 %cholesky.1244 = f32[128,128]{1,0:T(8,128)S(1)} custom-call(f32[128,128]{1,0:T(8,128)S(1)} %convolution_subtract_fusion.27), custom_call_target="Cholesky" | custom-call | tf_op jit(solution)/shard_map/while/body/eval_jaxpr/jit(cholesky)/cholesky | solution.py:114
  486.4 18.5 %while.45 = (s32[]{:T(128)}, f32[768,768]{0,1:T(8,128)}, s32[6,2]{0,1:T(2,128)S(1)}, f32[6,128,128]{2,1,0:T(8,128)S(1)}, s32[]{:T(128)}) while((s32[]{:T(128)}, f32[768,768]{0,1:T(8,128)}, s32[6,2]{0,1:T(2,128)S(1)}, f32[6,128,128]{2,1,0:T(8,128)S(1)}, s32[]{:T(128)}) %tuple.228), condition=%wide.while_cond.1, body=%wide.while_body.1.sunk | while | flops 2 | bytes 393321 | solution.py:124
  505.0 59.1 %custom-call.120 = f32[6,128,128]{1,2,0:T(8,128)S(1)} custom-call(f32[6,128,128]{2,1,0:T(8,128)S(1)} %get-tuple-element.702), custom_call_target="InvertDiagBlocksLowerTriangular" | custom-call | tf_op jit(solution)/shard_map/while/body/eval_jaxpr/jit(_solve_triangular)/triangular_solve | solution.py:124
  586.4 9.0 select_add_fusion.8
  602.5 41.8 %all_to_all.16 = f32[32,24,769]{2,1,0:T(8,128)S(1)} all-to-all(f32[32,24,769]{2,1,0:T(8,128)S(1)} %pad_maximum_fusion), channel_id=1, replica_groups=mesh['grp'=4,'blk_0'=4,'blk_1'=4,'blk_2'=2] {'blk_0','blk_1','blk_2'}, dimensions={0} | all-to-all | bytes 4724736 | tf_op jit(solution)/shard_map/all_to_all | solution.py:55
  644.8 10.6 all_to_all.17
  657.6 5.0 all-to-all-start.2
  663.7 34.3 %all-to-all-done.2 = f32[32,24,769]{2,1,0:T(8,128)S(1)} async-done(((f32[32,24,769]{2,1,0:T(8,128)}), f32[32,24,769]{2,1,0:T(8,128)S(1)}, u32[]{:S(2)}, u32[]{:S(2)}) %all-to-all-start.2) | async-done | bytes 2362400 | tf_op jit(solution)/shard_map/all_to_all | solution.py:71
  704.9 3.2 copy.153
  711.5 11.7 %cholesky.563 = f32[128,128]{1,0:T(8,128)S(1)} custom-call(f32[128,128]{1,0:T(8,128)S(1)} %cholesky.692), custom_call_target="Cholesky" | custom-call | tf_op jit(solution)/shard_map/jit(cholesky)/cholesky | solution.py:228
  724.6 9.8 custom-call.61
  737.2 11.7 %cholesky.582 = f32[128,128]{1,0:T(8,128)S(1)} custom-call(f32[128,128]{1,0:T(8,128)S(1)} %cholesky.696), custom_call_target="Cholesky" | custom-call | tf_op jit(solution)/shard_map/jit(cholesky)/cholesky | solution.py:228
  749.0 10.0 custom-call.62
  760.9 11.7 %cholesky.603 = f32[128,128]{1,0:T(8,128)S(1)} custom-call(f32[128,128]{1,0:T(8,128)S(1)} %cholesky.701), custom_call_target="Cholesky" | custom-call | tf_op jit(solution)/shard_map/jit(cholesky)/cholesky | solution.py:228
  773.3 9.8 custom-call.63
  785.0 12.1 %cholesky.622 = f32[128,128]{1,0:T(8,128)S(1)} custom-call(f32[128,128]{1,0:T(8,128)S(1)} %cholesky.706), custom_call_target="Cholesky" | custom-call | tf_op jit(solution)/shard_map/jit(cholesky)/cholesky | solution.py:228
  797.8 9.8 custom-call.64
  809.4 11.7 %cholesky.641 = f32[128,128]{1,0:T(8,128)S(1)} custom-call(f32[128,128]{1,0:T(8,128)S(1)} %cholesky.711), custom_call_target="Cholesky" | custom-call | tf_op jit(solution)/shard_map/jit(cholesky)/cholesky | solution.py:228
  821.8 9.8 custom-call.65
  833.1 11.9 %cholesky.658 = f32[128,128]{1,0:T(8,128)S(1)} custom-call(f32[128,128]{1,0:T(8,128)S(1)} %convolution_subtract_fusion.13), custom_call_target="Cholesky" | custom-call | tf_op jit(solution)/shard_map/jit(cholesky)/cholesky | solution.py:228
  851.9 20.9 %while.43 = (s32[]{:T(128)}, f32[768,768]{1,0:T(8,128)}, s32[6,2]{0,1:T(2,128)S(1)}, f32[6,128,128]{2,1,0:T(8,128)}, s32[]{:T(128)}) while((s32[]{:T(128)}, f32[768,768]{1,0:T(8,128)}, s32[6,2]{0,1:T(2,128)S(1)}, f32[6,128,128]{2,1,0:T(8,128)}, s32[]{:T(128)}) %tuple.237), condition=%wide.while_cond.2.clone, body=%wide.while_body.2.clone.sunk | while | flops 2 | bytes 132705 | solution.py:229
  852.6 2.9 bitcast_dynamic-update-slice_fusion.9
  856.1 2.9 bitcast_dynamic-update-slice_fusion.9
  859.6 2.9 bitcast_dynamic-update-slice_fusion.9
  866.6 2.9 bitcast_dynamic-update-slice_fusion.9
  872.9 59.8 %custom-call.67 = f32[6,128,128]{1,2,0:T(8,128)S(1)} custom-call(f32[6,128,128]{2,1,0:T(8,128)} %get-tuple-element.175), custom_call_target="InvertDiagBlocksLowerTriangular" | custom-call | tf_op jit(solution)/shard_map/jit(_cho_solve)/triangular_solve/custom-call.2 | solution.py:229
  949.1 195.3 %while.40 = (s32[]{:T(128)}, f32[2,768]{1,0:T(2,128)S(1)}, f32[2,768,768]{1,2,0:T(8,128)}, f32[2,768]{1,0:T(2,128)S(1)}, f32[2,768]{1,0:T(2,128)S(1)}, /*index=5...) while((s32[]{:T(128)}, f32[2,768]{1,0:T(2,128)S(1)}, f32[2,768,768]{1,2,0:T(8,128)}, ...), condition=%wide.region_17.21_spmd, body=%wide.region_16.20_spmd.sunk | while | flops 9445127 | bytes 17108324 | solution.py:162
  949.3 3.3 constant_dynamic-slice_fusion.8
  956.3 17.2 %while.44 = (s32[]{:T(128)}, f32[768,768]{1,0:T(8,128)}, s32[6,2]{0,1:T(2,128)S(1)}, f32[6,128,128]{2,1,0:T(8,128)S(1)}, s32[]{:T(128)}) while((s32[]{:T(128)}, f32[768,768]{1,0:T(8,128)}, s32[6,2]{0,1:T(2,128)S(1)}, f32[6,128,128]{2,1,0:T(8,128)S(1)}, s32[]{:T(128)}) %tuple.231), condition=%wide.while_cond.2, body=%wide.while_body.2.sunk | while | flops 2 | bytes 131181 | solution.py:160
  973.5 59.0 %custom-call.111 = f32[6,128,128]{1,2,0:T(8,128)S(1)} custom-call(f32[6,128,128]{2,1,0:T(8,128)S(1)} %get-tuple-element.665), custom_call_target="InvertDiagBlocksLowerTriangular" | custom-call | tf_op jit(solution)/shard_map/while/body/eval_jaxpr/jit(_solve_triangular)/triangular_solve/custom-call.2 | solution.py:160
  1046.9 3.3 constant_dynamic-slice_fusion.8
  1053.8 17.2 %while.44 = (s32[]{:T(128)}, f32[768,768]{1,0:T(8,128)}, s32[6,2]{0,1:T(2,128)S(1)}, f32[6,128,128]{2,1,0:T(8,128)S(1)}, s32[]{:T(128)}) while((s32[]{:T(128)}, f32[768,768]{1,0:T(8,128)}, s32[6,2]{0,1:T(2,128)S(1)}, f32[6,128,128]{2,1,0:T(8,128)S(1)}, s32[]{:T(128)}) %tuple.231), condition=%wide.while_cond.2, body=%wide.while_body.2.sunk | while | flops 2 | bytes 131181 | solution.py:160
  1071.1 59.0 %custom-call.111 = f32[6,128,128]{1,2,0:T(8,128)S(1)} custom-call(f32[6,128,128]{2,1,0:T(8,128)S(1)} %get-tuple-element.665), custom_call_target="InvertDiagBlocksLowerTriangular" | custom-call | tf_op jit(solution)/shard_map/while/body/eval_jaxpr/jit(_solve_triangular)/triangular_solve/custom-call.2 | solution.py:160
  (528 shorter events, 291.6 us)
Async XLA Ops:
  0.6 55.8 %copy-start = (f32[128,1536]{1,0:T(8,128)S(1)}, f32[128,1536]{1,0:T(8,128)}, u32[]{:S(2)}) copy-start(f32[128,1536]{1,0:T(8,128)} %param.31) | copy-start | bytes 2359300
  49.9 11.1 copy-start.17
  49.9 11.0 collective-permute-start
  57.9 3.1 collective-permute-start.4
  60.1 4.7 collective-permute-start.1
  60.4 2.4 collective-permute-start.2
  60.7 3.0 collective-permute-start.3
  60.9 4.9 copy-start.14
  62.4 2.2 collective-permute-start.5
  66.3 4.5 copy-start.6
  66.4 4.5 copy-start.10
  74.8 1.4 copy-start.2
  319.3 1.9 copy-start.8
  321.2 7.8 copy-start.9
  321.2 7.8 copy-start.7
  321.3 7.8 copy-start.11
  331.5 4.5 copy-start.6
  331.5 4.5 copy-start.10
  340.0 1.4 copy-start.2
  584.5 1.9 copy-start.8
  586.4 9.1 copy-start.9
  586.4 9.1 copy-start.7
  586.4 9.1 copy-start.11
  657.6 40.4 %all-to-all-start.2 = ((f32[32,24,769]{2,1,0:T(8,128)}), f32[32,24,769]{2,1,0:T(8,128)S(1)}, u32[]{:S(2)}, u32[]{:S(2)}) async-start(f32[32,24,769]{2,1,0:T(8,128)} %broadcast_in_dim.91), calls=%async_computation.2 | async-start | bytes 5505024 | tf_op jit(solution)/shard_map/all_to_all | solution.py:71
  698.0 1.6 copy-start.4
  701.2 2.1 copy-start.12
  710.0 1.5 copy-start.5
  850.3 1.6 copy-start.20
  850.3 82.3 %copy-start.13 = (f32[768]{0:T(1024)S(1)}, f32[768]{0:T(1024)}, u32[]{:S(2)}) copy-start(f32[768]{0:T(1024)} %param.34) | copy-start | bytes 9220
  851.9 95.1 %copy-start.3 = (f32[768,768]{1,0:T(8,128)S(1)}, f32[768,768]{1,0:T(8,128)}, u32[]{:S(2)}) copy-start(f32[768,768]{1,0:T(8,128)} %get-tuple-element.867) | copy-start | bytes 7077892
  935.4 13.7 %copy-start.16 = (f32[2,768]{1,0:T(2,128)S(1)}, f32[2,768]{1,0:T(2,128)}, u32[]{:S(2)}) copy-start(f32[2,768]{1,0:T(2,128)} %custom-call.80) | copy-start | bytes 18436
  949.1 196.4 %copy-start.15 = (f32[2]{0:T(128)S(1)}, f32[2]{0:T(128)}, u32[]{:S(2)}) copy-start(f32[2]{0:T(128)} %copy-done.14) | copy-start | bytes 28
  949.1 196.4 %copy-start.19 = (f32[2]{0:T(128)S(1)}, f32[2]{0:T(128)}, u32[]{:S(2)}) copy-start(f32[2]{0:T(128)} %add_convert_fusion) | copy-start | bytes 28
  949.1 197.2 %copy-start.18 = (f32[3]{0:T(128)S(1)}, f32[3]{0:T(128)}, u32[]{:S(2)}) copy-start(f32[3]{0:T(128)} %copy-done.17) | copy-start | bytes 40
  1144.5 2.7 copy-start.1
  1144.5 1.8 collective-permute-start.6
where the time goes:
time: 1160 us; the launch traced here: 1150 us
  other arithmetic  700 us (60%)
  matrix products  151 us (13%)
  local copies, waits for them, and re-layouts  137 us (12%)
  blocking collectives  77 us (7%)
  waiting for transfers between devices  34.4 us (3%)
  loops' own time  16.8 us (1%)
  starting transfers between devices  15.9 us (1%)
  between operations  15.3 us (1%)
    another operation x44, other arithmetic, factor_block(): return jnp.linalg.cholesky(kkt)  250 us
    another operation x22, other arithmetic, on_device(): schur_factor = jnp.linalg.cholesky(schur_matrix)  124 us
    another operation x6, other arithmetic, accumulate(): jax.scipy.linalg.solve_triangular(lower_factor, avail_row[:, None] * bord...  121 us
    another operation x8, other arithmetic, single(): jax.scipy.linalg.solve_triangular(lower_factor, halfway, lower=True, tran...  121 us
    another operation x5, other arithmetic, on_device(): jax.scipy.linalg.cho_solve((schur_factor, True), grad_total - first_rhs)  62.5 us
    all_to_all x1, blocking collectives, summed_on_arrival(): lax.all_to_all(pieces, axis, split_axis=0, concat_axis=0, tiled=True)  41.8 us
    another operation x60, local copies, waits for them, and re-layouts  36.6 us
    another operation x42, local copies, waits for them, and re-layouts, single(): jax.scipy.linalg.solve_triangular(lower_factor, halfway, lower=True, tran...  34.3 us
  transfers between devices with their start and end apart: 8, of which 2 were waited for; matrix products, arithmetic and copies ran while one was open for 1% of the time, Pallas kernels for 0%

commit v1 on v0

v1 whole, which is shorter than its diff:
```python
import functools

import jax
import jax.numpy as jnp
from jax import lax
from jax.experimental import pallas as pl
from jax.experimental.pallas import tpu as pltpu
from jax.sharding import Mesh
from jax.sharding import PartitionSpec as P

GRP_BLK = ("grp", "blk_0", "blk_1", "blk_2")
CHIPS = ("grp", "blk_0", "blk_1")
CORE = "blk_2"
HOURS = 2
TILE = 128
PANEL = 8
HIGHEST = lax.Precision.HIGHEST
F32 = jnp.float32
BF16 = jnp.bfloat16


def lanes_of(x, k):
    return jnp.broadcast_to(x[:, k : k + 1], x.shape)


def row_of(x, j):
    return jnp.broadcast_to(x[j : j + 1, :], x.shape)


def invert_tiles(refs):
    shape = (PANEL, TILE)
    lane = lax.broadcasted_iota(jnp.int32, shape, 1)
    sub = lax.broadcasted_iota(jnp.int32, shape, 0)
    panels = TILE // PANEL
    for t in range(panels):
        lo = PANEL * t
        inside = (lane >= lo) & (lane < lo + PANEL)
        eye = lane == sub + lo
        for ref in refs:
            tile = ref[...]
            rows = tile[lo : lo + PANEL, :]
            cols = [lanes_of(rows, lo + j) for j in range(PANEL)]
            rows = jnp.where(inside, jnp.where(eye, 1.0, 0.0), rows)
            for j in range(PANEL):
                own = sub == j
                inverse = 1.0 / row_of(cols[j], j)
                pivot = row_of(rows, j) * inverse
                col = cols[j]
                rows = jnp.where(own, pivot, rows - col * pivot)
                for q in range(j + 1, PANEL):
                    c = row_of(cols[q], j) * inverse
                    cols[q] = jnp.where(own, c, cols[q] - col * c)
            spread = [row_of(rows, j) for j in range(PANEL)]
            for s in range(1, panels):
                i = PANEL * ((t + s) % panels)
                other = tile[i : i + PANEL, :]
                acc = jnp.where(inside, 0.0, other)
                for j in range(PANEL):
                    acc = acc - lanes_of(other, lo + j) * spread[j]
                ref[i : i + PANEL, :] = acc
            ref[lo : lo + PANEL, :] = rows


def split(x):
    hi = x.astype(BF16)
    return hi, (x - hi.astype(F32)).astype(BF16)


def dot3(a, b):
    ah, al = split(a)
    bh, bl = split(b)
    return jnp.dot(
        jnp.concatenate([ah, ah, al], 1),
        jnp.concatenate([bh, bl, bh], 0),
        preferred_element_type=F32,
    )


def dot3_nt(a, b):
    ah, al = split(a)
    bh, bl = split(b)
    return lax.dot_general(
        jnp.concatenate([ah, ah, al], 1),
        jnp.concatenate([bh, bl, bh], 1),
        (((1,), (1,)), ((), ())),
        preferred_element_type=F32,
    )


def sweep_inverse(mats, tiles):
    count, n, _ = mats.shape

    def step(k, carry):
        at = pl.multiple_of(k * TILE, TILE)
        here = pl.ds(at, TILE)
        for m in range(count):
            tiles[m][...] = mats[m, here, here]
        invert_tiles([tiles[m] for m in range(count)])
        row = lax.broadcasted_iota(jnp.int32, (n, TILE), 0)
        pivot_rows = (row >= at) & (row < at + TILE)
        for m in range(count):
            inverse = tiles[m][...]
            mats[m, here, here] = jnp.zeros((TILE, TILE), F32)
            scaled = dot3(inverse, mats[m, here, :])
            column = mats[m, :, here]
            mats[m, :, here] = jnp.zeros((n, TILE), F32)
            mats[m, here, :] = scaled
            mats[m, here, here] = inverse
            mats[m] = mats[m] - dot3(jnp.where(pivot_rows, 0.0, column), mats[m, here, :])
        return carry

    lax.fori_loop(0, n // TILE, step, 0)


def as_column(row):
    n = row.shape[1]
    eye = lax.broadcasted_iota(jnp.int32, (TILE, TILE), 0) == lax.broadcasted_iota(
        jnp.int32, (TILE, TILE), 1
    )
    parts = []
    for t in range(0, n, TILE):
        wide = jnp.broadcast_to(row[:, t : t + TILE], (TILE, TILE))
        parts.append(jnp.sum(jnp.where(eye, wide, 0.0), axis=1, keepdims=True))
    return jnp.concatenate(parts, axis=0)


def hours_kernel(
    scale, diag, avail, avail_col, corrected_col, constraints, border, border_t,
    inverses, packed, solved, scaled, coupled, *tiles,
):
    nb = border.shape[0]
    wide = 256
    eye = lax.broadcasted_iota(jnp.int32, (TILE, TILE), 0) == lax.broadcasted_iota(
        jnp.int32, (TILE, TILE), 1
    )
    nt = (((1,), (1,)), ((), ()))
    for m in range(HOURS):
        scaled[...] = (constraints[...].astype(F32) * scale[m : m + 1, :]).astype(BF16)
        for c in range(0, nb, wide):
            both = lax.dot_general(
                scaled[...], constraints[c : c + wide, :], nt, preferred_element_type=F32
            ) + lax.dot_general(
                constraints[...], scaled[c : c + wide, :], nt, preferred_element_type=F32
            )
            inverses[m, :, c : c + wide] = 0.5 * both
        for c in range(0, nb, TILE):
            block = inverses[m, c : c + TILE, c : c + TILE]
            extra = jnp.where(eye, diag[m : m + 1, c : c + TILE], 0.0)
            inverses[m, c : c + TILE, c : c + TILE] = block + extra
    sweep_inverse(inverses, tiles)
    total = jnp.zeros((1, nb), F32)
    for m in range(HOURS):
        y = jnp.sum(corrected_col[:, m : m + 1] * inverses[m], axis=0, keepdims=True)
        solved[m : m + 1, :] = y
        total = total + avail[m : m + 1, :] * y
    gradient = jnp.sum(as_column(total) * border[...], axis=0, keepdims=True)
    middle = jnp.zeros((nb, nb), F32)
    for m in range(HOURS):
        middle = middle + inverses[m] * avail_col[:, m : m + 1] * avail[m : m + 1, :]
    coupled[...] = dot3_nt(middle, border_t[...])
    row = 0
    for i in range(0, nb, TILE):
        part = dot3(border_t[i : i + TILE, :], coupled[:, : i + TILE])
        for j in range(0, i + TILE, TILE):
            packed[row : row + TILE, :] = part[:, j : j + TILE]
            row += TILE
    packed[row:, :] = jnp.zeros((packed.shape[0] - row, TILE), F32)
    for t in range(nb // TILE):
        packed[row + t : row + t + 1, :] = gradient[:, t * TILE : (t + 1) * TILE]


def finish_kernel(
    packed, first_diag, first_rhs, border, avail_col, inverses, solved,
    first_step, steps, schur, *tiles,
):
    nb = border.shape[0]
    eye = lax.broadcasted_iota(jnp.int32, (TILE, TILE), 0) == lax.broadcasted_iota(
        jnp.int32, (TILE, TILE), 1
    )
    row = 0
    for i in range(0, nb, TILE):
        for j in range(0, i + TILE, TILE):
            block = packed[row : row + TILE, :]
            row += TILE
            if i == j:
                block = block + jnp.where(eye, first_diag[:, i : i + TILE], 0.0)
            else:
                schur[0, j : j + TILE, i : i + TILE] = block.T
            schur[0, i : i + TILE, j : j + TILE] = block
    sweep_inverse(schur, tiles)
    gradient = jnp.concatenate(
        [packed[row + t : row + t + 1, :] for t in range(nb // TILE)], axis=1
    )
    rhs = as_column(gradient - first_rhs[...])
    x = jnp.sum(rhs * schur[0], axis=0, keepdims=True)
    first_step[...] = x
    v = jnp.sum(border[...] * x, axis=1, keepdims=True)
    for m in range(HOURS):
        w = avail_col[:, m : m + 1] * v
        steps[m : m + 1, :] = solved[m : m + 1, :] - jnp.sum(
            w * inverses[m], axis=0, keepdims=True
        )


PARAMS = pltpu.CompilerParams(vmem_limit_bytes=56 * 2**20)


def tile_scratch(count):
    return [pltpu.VMEM((TILE, TILE), F32) for _ in range(count)]


def summed_over_all(array):
    rows, width = array.shape
    half = rows // 2
    core = lax.axis_index(CORE)
    chips = lax.axis_size(CHIPS)
    pair = [(0, 1), (1, 0)]
    kept = lax.dynamic_slice_in_dim(array, core * half, half, 0)
    sent = lax.dynamic_slice_in_dim(array, (1 - core) * half, half, 0)
    mine = kept + lax.ppermute(sent, CORE, pair)
    pieces = mine.reshape(chips, half // chips, width)
    piece = lax.all_to_all(pieces, CHIPS, 0, 0, tiled=True).sum(axis=0)
    spread = jnp.broadcast_to(piece[None], (chips, *piece.shape))
    mine = lax.all_to_all(spread, CHIPS, 0, 0, tiled=True).reshape(half, width)
    other = lax.ppermute(mine, CORE, pair)
    first = core == 0
    return jnp.concatenate([jnp.where(first, mine, other), jnp.where(first, other, mine)], axis=0)


def on_device(
    barrier_scale, regularizer, availability, block_rhs, primal, link_mask, counts,
    constraints, border, link_out, link_in, first_diag, first_rhs,
):
    nb = border.shape[0]
    nk = link_in.shape[1]
    count = counts[0]
    second = lax.axis_index(CORE) == 1
    devices = lax.axis_size(GRP_BLK)
    pair = [(0, 1), (1, 0)]
    mask = link_mask.astype(F32)
    state = lax.dot_general(
        primal, link_out, (((1,), (1,)), ((), ())), precision=HIGHEST, preferred_element_type=F32
    )
    two, three = count >= 2, count == 3
    last = jnp.where(three, state[2], jnp.where(two, state[1], state[0]))
    incoming = lax.ppermute(last, GRP_BLK, [(d, d + 1) for d in range(devices - 1)])
    fields = jnp.concatenate([barrier_scale, regularizer, availability, block_rhs, mask], axis=1)
    lent = jnp.where(second, fields[0], fields[2])
    message = lax.ppermute(jnp.concatenate([lent, state[1]]), CORE, pair)
    borrowed, borrowed_state = message[:-nk], message[-nk:]
    early = jnp.where(two, jnp.where(second & three, fields[1], fields[0]), borrowed)
    early = jnp.where(second, early, fields[0])
    late = jnp.where(two, fields[1], borrowed)
    late = jnp.where(second, jnp.where(three, fields[2], jnp.where(two, fields[1], fields[0])), late)
    early_state = jnp.where(three, state[0], jnp.where(two, incoming, borrowed_state))
    early_state = jnp.where(second, early_state, incoming)
    late_state = jnp.where(three, state[1], jnp.where(two, state[0], incoming))
    late_state = jnp.where(second, late_state, state[0])
    work = jnp.stack([early, late])
    nv = barrier_scale.shape[1]
    scale, diag, avail, rhs, active = jnp.split(
        work, [nv, nv + nb, nv + 2 * nb, nv + 3 * nb], axis=1
    )
    linked = active * jnp.stack([early_state, late_state])
    corrected = rhs + lax.dot_general(
        linked, link_in, (((1,), (1,)), ((), ())), precision=HIGHEST, preferred_element_type=F32
    )
    avail_col = avail.T
    rows = -(-(nb // TILE * (nb // TILE + 1) // 2 * TILE + 8) // (devices * 8)) * devices * 8
    inverses, packed, solved = pl.pallas_call(
        hours_kernel,
        out_shape=(
            jax.ShapeDtypeStruct((HOURS, nb, nb), F32),
            jax.ShapeDtypeStruct((rows, TILE), F32),
            jax.ShapeDtypeStruct((HOURS, nb), F32),
        ),
        scratch_shapes=[pltpu.VMEM((nb, nv), BF16), pltpu.VMEM((nb, nb), F32), *tile_scratch(HOURS)],
        compiler_params=PARAMS,
        name="hours",
    )(scale, diag, avail, avail_col, corrected.T, constraints, border, border.T)
    total = summed_over_all(packed)
    first_step, steps = pl.pallas_call(
        finish_kernel,
        out_shape=(jax.ShapeDtypeStruct((1, nb), F32), jax.ShapeDtypeStruct((HOURS, nb), F32)),
        scratch_shapes=[pltpu.VMEM((1, nb, nb), F32), *tile_scratch(1)],
        compiler_params=PARAMS,
        name="finish",
    )(total, first_diag[None], first_rhs[None], border, avail_col, inverses, solved)
    returned = lax.ppermute(jnp.where(second, steps[0], steps[1]), CORE, pair)
    zero = jnp.zeros((nb,), F32)
    slot_0 = jnp.where(second, jnp.where(three, returned, jnp.where(two, steps[0], steps[1])), steps[0])
    slot_1 = jnp.where(two, jnp.where(second & three, steps[0], steps[1]), zero)
    slot_2 = jnp.where(three, jnp.where(second, steps[1], returned), zero)
    return jnp.stack([slot_0, slot_1, slot_2]), first_step[0]


def solution(mesh):
    split_mesh = Mesh(mesh.devices.reshape(mesh.shape["grp"], 4, 4, 2), GRP_BLK)
    whole = P(GRP_BLK, None)
    placed = (whole,) * 6 + (P(GRP_BLK),) + (P(),) * 6
    return jax.shard_map(
        on_device, mesh=split_mesh, in_specs=placed, out_specs=(whole, P()), check_vma=False
    )
```

time: 1160 us -> 192 us (0.17); the launches traced: 1150 us -> 192 us
  other arithmetic: 700 us -> 6.19 us
  matrix products: 151 us -> 1.85 us
  local copies, waits for them, and re-layouts: 137 us -> 11.7 us
  Pallas kernels: 0 us -> 115 us
  blocking collectives: 77 us -> 44.1 us
  waiting for transfers between devices: 34.4 us -> 3.23 us
  loops' own time: 16.8 us -> 0 us
  between operations: 15.3 us -> 1.44 us
    another operation x85 -> x4, other arithmetic: 678 us -> 1.83 us  [the longest x2 1.22 us: on_device(): work = jnp.stack([early, late])]
    pallas_call x0 -> x2, Pallas kernels: none -> 115 us  [the longest x1 77.9 us: on_device(): pl.pallas_call(hours_kernel, out_shape=(jax.ShapeDtypeStruct((HOURS, nb,...]
    another operation x140 -> x0, matrix products: 114 us -> none  [the longest x22 24.2 us: accumulate(): jax.scipy.linalg.solve_triangular(lower_factor, avail_row[:, None] * bord...]
    another operation x169 -> x4, local copies, waits for them, and re-layouts: 93.9 us -> 0.04 us  [the longest x2 0.03 us: on_device(): work = jnp.stack([early, late])]
    all_to_all x1 -> x0, waiting for transfers between devices: 34.3 us -> none  [sent_to_all(): lax.all_to_all(jnp.broadcast_to(array[None], (length, *array.shape)), axi...]
    dot_general x12 -> x0, matrix products: 34.1 us -> none  [the longest x2 16.9 us: accumulate(): lax.dot_general(solved, solved, (((0,), (0,)), ((), ())), precision=HIGHE...]
    unnamed x4 -> x0, blocking collectives: 24.6 us -> none
    another operation x7 -> x0, loops' own time: 16.8 us -> none  [the longest x1 15.8 us: schur_terms(): lax.scan(accumulate, initial, (barrier_scale, regularizer, availability,...]
  transfers between devices with their start and end apart: 8 -> 5, of which waited for: 2 -> 2; matrix products, arithmetic and copies ran while one was open for 1% -> 4% of each run, Pallas kernels for 0% -> 0%
where the time goes in v1:
time: 192 us
  Pallas kernels  115 us (60%)
  blocking collectives  44.1 us (23%)
  local copies, waits for them, and re-layouts  11.7 us (6%)
  starting transfers between devices  8.24 us (4%)
  other arithmetic  6.19 us (3%)
  waiting for transfers between devices  3.23 us (2%)
    pallas_call x1, Pallas kernels, on_device(): pl.pallas_call(hours_kernel, out_shape=(jax.ShapeDtypeStruct((HOURS, nb,...  77.9 us
    pallas_call x1, Pallas kernels, on_device(): pl.pallas_call(finish_kernel, out_shape=(jax.ShapeDtypeStruct((1, nb), F3...  37 us
    all_to_all x1, blocking collectives, summed_over_all(): piece = lax.all_to_all(pieces, CHIPS, 0, 0, tiled=True).sum(axis=0)  25.8 us
    all_to_all x1, blocking collectives, summed_over_all(): mine = lax.all_to_all(spread, CHIPS, 0, 0, tiled=True).reshape(half, width)  18.3 us
    unnamed x18, local copies, waits for them, and re-layouts  7.09 us
  transfers between devices with their start and end apart: 5, of which 2 were waited for; matrix products, arithmetic and copies ran while one was open for 4% of the time, Pallas kernels for 0%

profile of v1, /device:TPU:1, one launch (start us, length us, event | category | flops | bytes accessed | tf_op | source)
XLA Modules:
  0.0 191.6 jit_solution(177314163637801775)
XLA Ops:
  0.6 0.0 copy-start
  0.6 0.8 constant_dynamic-update-slice_fusion.4
  1.5 0.7 constant_dynamic-update-slice_fusion.3
  2.2 0.7 constant_dynamic-update-slice_fusion.2
  2.9 0.7 constant_dynamic-update-slice_fusion.1
  3.6 0.7 constant_dynamic-update-slice_fusion
  4.3 0.1 slice_reduce_fusion
  4.4 0.0 copy-done
  4.4 1.4 fusion.13
  5.9 1.5 collective-permute-start
  8.1 3.2 %collective-permute-start.1 = (f32[128]{0:T(128)S(1)}, f32[128]{0:T(128)S(1)}, u32[]{:S(2)}, u32[]{:S(2)}) collective-permute-start(f32[128]{0:T(128)S(1)} %broadcast_select_fusion.11), channel_id=1, source_target_pairs={{0,1},{1,2},{2,3},{3,4},{4,5},{5,6},{6,7},{7,8},{8,9},{9,10},{10,1... | collective-permute-start | bytes 1544 | tf_op jit(solution)/shard_map/ppermute | solution.py:246
  11.3 0.0 copy-start.2
  11.3 3.1 %copy.38 = f32[768,768]{0,1:T(8,128)} copy(f32[768,768]{1,0:T(8,128)} %border.3) | data formatting | bytes 4718592 | tf_op args[8]
  14.4 0.0 collective-permute-done
  14.5 0.6 fusion.scale
  15.1 0.6 fusion.3
  15.7 0.0 copy-start.3
  15.7 0.0 collective-permute-done.1
  15.7 0.0 copy-done.2
  15.7 0.4 convolution_add_fusion
  16.1 1.0 copy.37
  17.2 1.0 copy.40
  18.1 0.0 copy-done.3
  18.1 77.9 %hours.1 = (f32[2,768,768]{2,1,0:T(8,128)}, f32[3072,128]{1,0:T(8,128)}, f32[2,768]{1,0:T(2,128)}) custom-call(f32[2,1536]{1,0:T(2,128)} %fusion.scale, f32[2,768]{1,0:T(2,128)} %get-tuple-element.22.diag, f32[2,768]{1,0:T(2,128)} %copy-done.3, f32[768,2]{1,0:T(8,128)} %bitcast.29, f32[768,2]{1,0:T(8,128)} %bitcast.33, bf16[768,1536]{1,0:T(8,128)(2,1)} %constraints.1, ...), custom_call_target="tpu_custom_call" | custom-call | tf_op jit(solution)/shard_map/hours/pallas_call | solution.py:270
  96.0 0.0 copy-start.1
  96.0 2.2 %constant_dynamic-slice_fusion = f32[1536,128]{1,0:T(8,128)} fusion(f32[3072,128]{1,0:T(8,128)} %get-tuple-element.7, s32[]{:T(128)S(6)} %select_n.173), kind=kLoop, calls=%fused_computation.54 | loop fusion | bytes 1572868 | tf_op jit(solution)/shard_map/dynamic_slice | solution.py:219
  98.2 0.0 collective-permute-start.2
  98.2 2.5 %collective-permute-done.2 = f32[1536,128]{1,0:T(8,128)S(1)} collective-permute-done((f32[1536,128]{1,0:T(8,128)}, f32[1536,128]{1,0:T(8,128)S(1)}, u32[]{:S(2)}, u32[]{:S(2)}) %collective-permute-start.2) | collective-permute-done | bytes 786464 | tf_op jit(solution)/shard_map/ppermute | solution.py:220
  100.7 0.0 copy-done.1
  100.7 0.1 dynamic-slice_add_fusion
  100.8 25.8 %all_to_all.10 = f32[64,24,128]{2,1,0:T(8,128)S(1)} all-to-all(f32[64,24,128]{2,1,0:T(8,128)S(1)} %bitcast.31), channel_id=1, replica_groups=mesh['grp'=4,'blk_0'=4,'blk_1'=4,'blk_2'=2] {'grp','blk_0','blk_1'}, dimensions={0} | all-to-all | bytes 1572864 | tf_op jit(solution)/shard_map/all_to_all | solution.py:222
  126.6 0.0 copy-start.4
  126.6 0.0 copy-start.5
  126.6 0.1 reduce_sum.9
  126.7 0.1 broadcast_in_dim.17
  126.7 18.3 %all_to_all.11 = f32[64,24,128]{2,1,0:T(8,128)S(1)} all-to-all(f32[64,24,128]{2,1,0:T(8,128)S(1)} %broadcast_in_dim.17), channel_id=1, replica_groups=mesh['grp'=4,'blk_0'=4,'blk_1'=4,'blk_2'=2] {'grp','blk_0','blk_1'}, dimensions={0} | all-to-all | bytes 1572864 | tf_op jit(solution)/shard_map/all_to_all | solution.py:224
  145.0 3.1 %collective-permute-start.3 = (f32[1536,128]{1,0:T(8,128)S(1)}, f32[1536,128]{1,0:T(8,128)S(1)}, u32[]{:S(2)}, u32[]{:S(2)}) collective-permute-start(f32[1536,128]{1,0:T(8,128)S(1)} %bitcast.32), channel_id=1, source_target_pairs={{0,1},{1,0},{2,3},{3,2},{4,5},{5,4},{6,7},{7,6},{8,9},{9,8},{10,11... | collective-permute-start | bytes 2359304 | tf_op jit(solution)/shard_map/ppermute | solution.py:225
  148.1 0.0 copy-done.4
  148.1 0.6 broadcast_in_dim.18.first_diag
  148.7 0.0 copy-done.5
  148.7 0.6 broadcast_in_dim.19.first_rhs
  149.3 0.7 collective-permute-done.3
  150.0 0.1 broadcast_select_fusion.1
  150.2 1.3 pad_maximum_fusion.packed
  151.4 37.0 %finish.1 = (f32[1,768]{1,0:T(1,128)}, f32[2,768]{1,0:T(2,128)}) custom-call(f32[3072,128]{1,0:T(8,128)} %pad_maximum_fusion.packed, f32[1,768]{1,0:T(1,128)} %broadcast_in_dim.18.first_diag, f32[1,768]{1,0:T(1,128)} %broadcast_in_dim.19.first_rhs, f32[768,768]{1,0:T(8,128)} %border.3, f32[768,2]{1,0:T(8,128)} %bitcast.30, ...), custom_call_target="tpu_custom_call" | custom-call | tf_op jit(solution)/shard_map/finish/pallas_call | solution.py:282
  188.4 0.8 slice_reduce_fusion.4
  189.2 0.4 collective-permute-start.4
  189.7 1.3 reduce.5
  191.0 0.0 collective-permute-done.4
  191.0 0.6 pad_maximum_fusion.2
  (12 shorter events, 0.1 us)
Async XLA Ops:
  0.6 3.8 %copy-start = (f32[128,1536]{1,0:T(8,128)S(1)}, f32[128,1536]{1,0:T(8,128)}, u32[]{:S(2)}) copy-start(f32[128,1536]{1,0:T(8,128)} %param.22) | copy-start | bytes 2359300
  5.9 8.5 %collective-permute-start = (f32[4096]{0:T(1024)S(1)}, f32[4096]{0:T(1024)S(1)}, u32[]{:S(2)}, u32[]{:S(2)}) collective-permute-start(f32[4096]{0:T(1024)S(1)} %pad_maximum_fusion.1), channel_id=1, source_target_pairs={{0,1},{1,0},{2,3},{3,2},{4,5},{5,4},{6,7},{7,6},{8,9},{9,8},{10,11... | collective-permute-start | bytes 49160 | tf_op jit(solution)/shard_map/ppermute | solution.py:249
  8.1 7.7 %collective-permute-start.1 = (f32[128]{0:T(128)S(1)}, f32[128]{0:T(128)S(1)}, u32[]{:S(2)}, u32[]{:S(2)}) collective-permute-start(f32[128]{0:T(128)S(1)} %broadcast_select_fusion.11), channel_id=1, source_target_pairs={{0,1},{1,2},{2,3},{3,4},{4,5},{5,6},{6,7},{7,8},{8,9},{9,10},{10,1... | collective-permute-start | bytes 1544 | tf_op jit(solution)/shard_map/ppermute | solution.py:246
  11.3 4.4 %copy-start.2 = (f32[768,128]{1,0:T(8,128)S(1)}, f32[768,128]{1,0:T(8,128)}, u32[]{:S(2)}) copy-start(f32[768,128]{1,0:T(8,128)} %param.23) | copy-start | bytes 1179652
  15.7 2.4 %copy-start.3 = (f32[2,768]{1,0:T(2,128)}, f32[2,768]{1,0:T(2,128)S(1)}, u32[]{:S(2)}) copy-start(f32[2,768]{1,0:T(2,128)S(1)} %get-tuple-element.21.avail) | copy-start | bytes 18436
  96.0 4.7 %copy-start.1 = (f32[3072,128]{1,0:T(8,128)S(1)}, f32[3072,128]{1,0:T(8,128)}, u32[]{:S(2)}) copy-start(f32[3072,128]{1,0:T(8,128)} %get-tuple-element.7) | copy-start | bytes 4718596
  98.2 2.5 %collective-permute-start.2 = (f32[1536,128]{1,0:T(8,128)}, f32[1536,128]{1,0:T(8,128)S(1)}, u32[]{:S(2)}, u32[]{:S(2)}) collective-permute-start(f32[1536,128]{1,0:T(8,128)} %constant_dynamic-slice_fusion), channel_id=1, source_target_pairs={{0,1},{1,0},{2,3},{3,2},{4,5},{5,4},{6,7},{7,6},{8,9},{9,8},{10,11... | collective-permute-start | bytes 2359304 | tf_op jit(solution)/shard_map/ppermute | solution.py:220
  126.6 21.6 %copy-start.4 = (f32[768]{0:T(1024)S(1)}, f32[768]{0:T(1024)}, u32[]{:S(2)}) copy-start(f32[768]{0:T(1024)} %param.24) | copy-start | bytes 9220
  126.6 22.1 %copy-start.5 = (f32[768]{0:T(1024)S(1)}, f32[768]{0:T(1024)}, u32[]{:S(2)}) copy-start(f32[768]{0:T(1024)} %param.25) | copy-start | bytes 9220
  145.0 5.0 %collective-permute-start.3 = (f32[1536,128]{1,0:T(8,128)S(1)}, f32[1536,128]{1,0:T(8,128)S(1)}, u32[]{:S(2)}, u32[]{:S(2)}) collective-permute-start(f32[1536,128]{1,0:T(8,128)S(1)} %bitcast.32), channel_id=1, source_target_pairs={{0,1},{1,0},{2,3},{3,2},{4,5},{5,4},{6,7},{7,6},{8,9},{9,8},{10,11... | collective-permute-start | bytes 2359304 | tf_op jit(solution)/shard_map/ppermute | solution.py:225
  189.2 1.7 collective-permute-start.4

commit v2 on v1

v2 whole, which is shorter than its diff:
```python
import functools

import jax
import jax.numpy as jnp
from jax import lax
from jax.experimental import pallas as pl
from jax.experimental.pallas import tpu as pltpu
from jax.sharding import Mesh
from jax.sharding import PartitionSpec as P

GRP_BLK = ("grp", "blk_0", "blk_1", "blk_2")
CHIPS = ("grp", "blk_0", "blk_1")
CORE = "blk_2"
HOURS = 2
TILE = 128
PANEL = 8
HIGHEST = lax.Precision.HIGHEST
CHUNK = 256
F32 = jnp.float32
BF16 = jnp.bfloat16
NT = (((1,), (1,)), ((), ()))


def lanes_of(x, k):
    return jnp.broadcast_to(x[:, k : k + 1], x.shape)


def row_of(x, j):
    return jnp.broadcast_to(x[j : j + 1, :], x.shape)


def invert_tiles(refs, reach, work=()):
    work = list(work)
    done = 0
    shape = (PANEL, TILE)
    lane = lax.broadcasted_iota(jnp.int32, shape, 1)
    sub = lax.broadcasted_iota(jnp.int32, shape, 0)
    panels = TILE // PANEL
    groups = reach // PANEL
    each = range(len(refs))
    for base in range(0, TILE, reach):
        parts = [
            [ref[base + PANEL * g : base + PANEL * (g + 1), :] for g in range(groups)]
            for ref in refs
        ]
        before = [ref[...] for ref in refs] if reach < TILE else None
        for t in range(groups):
            lo = base + PANEL * t
            inside = (lane >= lo) & (lane < lo + PANEL)
            eye = lane == sub + lo
            rows = [parts[m][t] for m in each]
            cols = [[lanes_of(rows[m], lo + j) for j in range(PANEL)] for m in each]
            rows = [jnp.where(inside, jnp.where(eye, 1.0, 0.0), rows[m]) for m in each]
            for j in range(PANEL):
                own = sub == j
                inverse = [1.0 / row_of(cols[m][j], j) for m in each]
                pivot = [row_of(rows[m], j) * inverse[m] for m in each]
                col = [cols[m][j] for m in each]
                for q in range(j + 1, PANEL):
                    for m in each:
                        c = row_of(cols[m][q], j) * inverse[m]
                        cols[m][q] = jnp.where(own, c, cols[m][q] - col[m] * c)
                rows = [jnp.where(own, pivot[m], rows[m] - col[m] * pivot[m]) for m in each]
            others = [(t + s) % groups for s in range(1, groups)]
            for m in each:
                spread = [row_of(rows[m], j) for j in range(PANEL)]
                acc = {i: jnp.where(inside, 0.0, parts[m][i]) for i in others}
                for i in others[:1]:
                    for j in range(PANEL):
                        acc[i] = acc[i] - lanes_of(parts[m][i], lo + j) * spread[j]
                for j in range(PANEL):
                    for i in others[1:]:
                        acc[i] = acc[i] - lanes_of(parts[m][i], lo + j) * spread[j]
                for i in others:
                    parts[m][i] = acc[i]
                parts[m][t] = rows[m]
            past = lo // PANEL + 1
            while done < len(work) and done * panels < past * len(work):
                work[done]()
                done += 1
        if reach == TILE:
            for m in each:
                for g in range(groups):
                    refs[m][PANEL * g : PANEL * (g + 1), :] = parts[m][g]
            continue
        wide = lax.broadcasted_iota(jnp.int32, (TILE, TILE), 1)
        tall = lax.broadcasted_iota(jnp.int32, (TILE, TILE), 0)
        own_lanes = (wide >= base) & (wide < base + reach)
        own_rows = (tall >= base) & (tall < base + reach)
        for m in each:
            block = list(parts[m])
            if base:
                block.insert(0, jnp.zeros((base, TILE), F32))
            if base + reach < TILE:
                block.append(jnp.zeros((TILE - base - reach, TILE), F32))
            block = jnp.concatenate(block, axis=0)
            bh, bl = split(block)
            xh, xl = split(before[m])
            change = mm(jnp.concatenate([xh, xl], 1), jnp.concatenate([bh, bh], 0)) + mm(xh, bl)
            rest = jnp.where(own_lanes, 0.0, before[m]) - change
            refs[m][...] = jnp.where(own_rows, block, rest)


def mm(a, b):
    return jnp.dot(a, b, preferred_element_type=F32)


def split(x):
    hi = x.astype(BF16)
    return hi, (x - hi.astype(F32)).astype(BF16)


def left(x):
    h, l = split(x)
    return jnp.concatenate([h, h, l], 1)


def right(x):
    h, l = split(x)
    return jnp.concatenate([h, l, h], 0)


def dot3(a, b):
    return mm(left(a), right(b))


def dot3_nt(a, b):
    h, l = split(b)
    return lax.dot_general(
        left(a), jnp.concatenate([h, l, h], 1), NT, preferred_element_type=F32
    )


def sweep_inverse(mats, tiles, columns, rows, reach, woven):
    count, n, _ = mats.shape
    each = range(count)
    last = n // TILE - 1

    def begin(k):
        at = pl.multiple_of(k * TILE, TILE)
        here = pl.ds(at, TILE)
        row = lax.broadcasted_iota(jnp.int32, (n, TILE), 0)
        pivot_rows = (row >= at) & (row < at + TILE)
        for m in each:
            inverse = tiles[m][...]
            scaled = dot3(inverse, mats[m, here, :])
            columns[m] = left(jnp.where(pivot_rows, 0.0, mats[m, :, here]))
            mats[m, :, here] = jnp.zeros((n, TILE), F32)
            mats[m, here, :] = scaled
            mats[m, here, here] = inverse
            rows[m] = right(mats[m, here, :])

    def update(m, c):
        at = slice(c, c + CHUNK)
        mats[m, :, at] = mats[m, :, at] - mm(columns[m], rows[m, :, at])

    work = [functools.partial(update, m, c) for c in range(0, n, CHUNK) for m in each]

    def step(k, carry):
        begin(k)
        after = pl.ds(pl.multiple_of((k + 1) * TILE, TILE), TILE)
        for m in each:
            tiles[m][...] = mats[m, after, after] - mm(columns[m, after, :], rows[m, :, after])
        invert_tiles([tiles[m] for m in each], reach, work if woven else ())
        if not woven:
            for item in work:
                item()
        return carry

    for m in each:
        tiles[m][...] = mats[m, :TILE, :TILE]
    invert_tiles([tiles[m] for m in each], reach)
    lax.fori_loop(0, last, step, 0)
    begin(last)
    for item in work:
        item()


def as_column(row):
    n = row.shape[1]
    eye = lax.broadcasted_iota(jnp.int32, (TILE, TILE), 0) == lax.broadcasted_iota(
        jnp.int32, (TILE, TILE), 1
    )
    parts = []
    for t in range(0, n, TILE):
        wide = jnp.broadcast_to(row[:, t : t + TILE], (TILE, TILE))
        parts.append(jnp.sum(jnp.where(eye, wide, 0.0), axis=1, keepdims=True))
    return jnp.concatenate(parts, axis=0)


def diagonal():
    return lax.broadcasted_iota(jnp.int32, (TILE, TILE), 0) == lax.broadcasted_iota(
        jnp.int32, (TILE, TILE), 1
    )


def hours_kernel(
    place, barrier_scale, regularizer, availability, block_rhs, link_mask, state, incoming, message,
    link_in, constraints, border_hbm, border_t_hbm,
    inverses_hbm, packed, solved, avail,
    inverses, border, border_t, scaled, coupled, columns, rows, sems, *tiles,
):
    nb, nv = constraints.shape
    nk = link_in.shape[1]
    loads = [
        pltpu.make_async_copy(border_hbm, border, sems.at[0]),
        pltpu.make_async_copy(border_t_hbm, border_t, sems.at[1]),
    ]
    for load in loads:
        load.start()
    count, second = place[0], place[1] == 1
    two, three = count >= 2, count == 3
    eye = diagonal()

    def early_late(field, at):
        own = [field[s : s + 1, :].astype(F32) for s in range(3)]
        borrowed = message[:, at : at + field.shape[1]]
        early = jnp.where(two, jnp.where(second & three, own[1], own[0]), borrowed)
        early = jnp.where(second, early, own[0])
        late = jnp.where(three, own[2], jnp.where(two, own[1], own[0]))
        late = jnp.where(second, late, jnp.where(two, own[1], borrowed))
        return early, late

    scale = early_late(barrier_scale, 0)
    diag = early_late(regularizer, nv)
    for m in range(HOURS):
        scaled[...] = (constraints[...].astype(F32) * scale[m]).astype(BF16)
        for c in range(0, nb, CHUNK):
            both = lax.dot_general(
                scaled[...], constraints[c : c + CHUNK, :], NT, preferred_element_type=F32
            ) + lax.dot_general(
                constraints[...], scaled[c : c + CHUNK, :], NT, preferred_element_type=F32
            )
            inverses[m, :, c : c + CHUNK] = 0.5 * both
        for c in range(0, nb, TILE):
            block = inverses[m, c : c + TILE, c : c + TILE]
            extra = jnp.where(eye, diag[m][:, c : c + TILE], 0.0)
            inverses[m, c : c + TILE, c : c + TILE] = block + extra
    sweep_inverse(inverses, tiles, columns, rows, 64, True)
    store = pltpu.make_async_copy(inverses, inverses_hbm, sems.at[2])
    store.start()
    own_state = [state[s : s + 1, :] for s in range(3)]
    arrived = incoming[...]
    given = message[:, nv + 3 * nb + nk :]
    early_state = jnp.where(three, own_state[0], jnp.where(two, arrived, given))
    early_state = jnp.where(second, early_state, arrived)
    late_state = jnp.where(three, own_state[1], jnp.where(two, own_state[0], arrived))
    late_state = jnp.where(second, late_state, own_state[0])
    active = early_late(link_mask, nv + 3 * nb)
    linked = jnp.concatenate(
        [active[0] * early_state, active[1] * late_state, jnp.zeros((6, nk), F32)], axis=0
    )
    links = dot3_nt(linked, link_in[...])
    rhs = early_late(block_rhs, nv + 2 * nb)
    available = early_late(availability, nv + nb)
    total = jnp.zeros((1, nb), F32)
    for m in range(HOURS):
        avail[m : m + 1, :] = available[m]
        corrected = as_column(rhs[m] + links[m : m + 1, :])
        y = jnp.sum(corrected * inverses[m], axis=0, keepdims=True)
        solved[m : m + 1, :] = y
        total = total + available[m] * y
    middle = jnp.zeros((nb, nb), F32)
    for m in range(HOURS):
        middle = middle + inverses[m] * as_column(available[m]) * available[m]
    for load in loads:
        load.wait()
    gradient = jnp.sum(as_column(total) * border[...], axis=0, keepdims=True)
    coupled[...] = dot3_nt(middle, border_t[...])
    row = 0
    for i in range(0, nb, TILE):
        part = dot3(border_t[i : i + TILE, :], coupled[:, : i + TILE])
        for j in range(0, i + TILE, TILE):
            packed[row : row + TILE, :] = part[:, j : j + TILE]
            row += TILE
    packed[row:, :] = jnp.zeros((packed.shape[0] - row, TILE), F32)
    for t in range(nb // TILE):
        packed[row + t : row + t + 1, :] = gradient[:, t * TILE : (t + 1) * TILE]
    store.wait()


def finish_kernel(
    place, packed, first_diag, first_rhs, avail, solved, border_hbm, inverses_hbm,
    first_step, steps, sent,
    schur, border, inverses, columns, rows, sems, *tiles,
):
    nb = schur.shape[1]
    loads = [
        pltpu.make_async_copy(border_hbm, border, sems.at[0]),
        pltpu.make_async_copy(inverses_hbm, inverses, sems.at[1]),
    ]
    for load in loads:
        load.start()
    eye = diagonal()
    row = 0
    for i in range(0, nb, TILE):
        for j in range(0, i + TILE, TILE):
            block = packed[row : row + TILE, :]
            row += TILE
            if i == j:
                block = block + jnp.where(eye, first_diag[:, i : i + TILE], 0.0)
            else:
                schur[0, j : j + TILE, i : i + TILE] = block.T
            schur[0, i : i + TILE, j : j + TILE] = block
    sweep_inverse(schur, tiles, columns, rows, TILE, False)
    gradient = jnp.concatenate(
        [packed[row + t : row + t + 1, :] for t in range(nb // TILE)], axis=1
    )
    rhs = as_column(gradient - first_rhs[...])
    x = jnp.sum(rhs * schur[0], axis=0, keepdims=True)
    first_step[...] = x
    for load in loads:
        load.wait()
    v = jnp.sum(border[...] * x, axis=1, keepdims=True)
    for m in range(HOURS):
        w = as_column(avail[m : m + 1, :]) * v
        steps[m : m + 1, :] = solved[m : m + 1, :] - jnp.sum(
            w * inverses[m], axis=0, keepdims=True
        )
    sent[...] = jnp.where(place[1] == 1, steps[0:1, :], steps[1:2, :])


PARAMS = pltpu.CompilerParams(vmem_limit_bytes=56 * 2**20)


def sweep_scratch(count, n):
    return [
        pltpu.VMEM((count, n, 3 * TILE), BF16),
        pltpu.VMEM((count, 3 * TILE, n), BF16),
        pltpu.SemaphoreType.DMA((3,)),
        *(pltpu.VMEM((TILE, TILE), F32) for _ in range(count)),
    ]


def spaces(count, scalar, remote):
    return [
        pl.BlockSpec(
            memory_space=pltpu.SMEM if k in scalar else pl.ANY if k in remote else pltpu.VMEM
        )
        for k in range(count)
    ]


def summed_over_all(array):
    rows, width = array.shape
    half = rows // 2
    core = lax.axis_index(CORE)
    chips = lax.axis_size(CHIPS)
    pair = [(0, 1), (1, 0)]
    kept = lax.dynamic_slice_in_dim(array, core * half, half, 0)
    sent = lax.dynamic_slice_in_dim(array, (1 - core) * half, half, 0)
    mine = kept + lax.ppermute(sent, CORE, pair)
    pieces = mine.reshape(chips, half // chips, width)
    piece = lax.all_to_all(pieces, CHIPS, 0, 0, tiled=True).sum(axis=0)
    spread = jnp.broadcast_to(piece[None], (chips, *piece.shape))
    mine = lax.all_to_all(spread, CHIPS, 0, 0, tiled=True).reshape(half, width)
    other = lax.ppermute(mine, CORE, pair)
    first = core == 0
    return jnp.concatenate([jnp.where(first, mine, other), jnp.where(first, other, mine)], axis=0)


def on_device(
    barrier_scale, regularizer, availability, block_rhs, primal, link_mask, counts,
    constraints, border, link_out, link_in, first_diag, first_rhs,
):
    nb, nv = constraints.shape
    count = counts[0]
    core = lax.axis_index(CORE)
    second = core == 1
    devices = lax.axis_size(GRP_BLK)
    pair = [(0, 1), (1, 0)]
    place = jnp.stack([count, core])
    state = lax.dot_general(
        primal, link_out, NT, precision=HIGHEST, preferred_element_type=F32
    )
    two, three = count >= 2, count == 3
    last = jnp.where(three, state[2:], jnp.where(two, state[1:2], state[:1]))
    incoming = lax.ppermute(last, GRP_BLK, [(d, d + 1) for d in range(devices - 1)])
    fields = (barrier_scale, regularizer, availability, block_rhs, link_mask.astype(F32))
    lent = [jnp.where(second, field[:1], field[2:]) for field in fields]
    message = lax.ppermute(jnp.concatenate([*lent, state[1:2]], axis=1), CORE, pair)
    packed_rows = (nb // TILE) * (nb // TILE + 1) // 2 * TILE + 8
    packed_rows = -(-packed_rows // (devices * 8)) * devices * 8
    square = pltpu.VMEM((nb, nb), F32)
    pairs = pltpu.VMEM((HOURS, nb, nb), F32)
    inverses, packed, solved, avail = pl.pallas_call(
        hours_kernel,
        out_shape=(
            jax.ShapeDtypeStruct((HOURS, nb, nb), F32),
            jax.ShapeDtypeStruct((packed_rows, TILE), F32),
            jax.ShapeDtypeStruct((HOURS, nb), F32),
            jax.ShapeDtypeStruct((HOURS, nb), F32),
        ),
        in_specs=spaces(13, (0,), (11, 12)),
        out_specs=spaces(4, (), (0,)),
        scratch_shapes=[
            pairs, square, square, pltpu.VMEM((nb, nv), BF16), square, *sweep_scratch(HOURS, nb)
        ],
        compiler_params=PARAMS,
        name="hours",
    )(
        place, barrier_scale, regularizer, availability, block_rhs, link_mask, state, incoming,
        message, link_in, constraints, border, border.T,
    )
    total = summed_over_all(packed)
    first_step, steps, sent = pl.pallas_call(
        finish_kernel,
        out_shape=(
            jax.ShapeDtypeStruct((1, nb), F32),
            jax.ShapeDtypeStruct((HOURS, nb), F32),
            jax.ShapeDtypeStruct((1, nb), F32),
        ),
        in_specs=spaces(8, (0,), (6, 7)),
        scratch_shapes=[pltpu.VMEM((1, nb, nb), F32), square, pairs, *sweep_scratch(1, nb)],
        compiler_params=PARAMS,
        name="finish",
    )(place, total, first_diag[None], first_rhs[None], avail, solved, border, inverses)
    returned = lax.ppermute(sent, CORE, pair)
    slot = jnp.arange(3, dtype=jnp.int32)[:, None]
    lead = jnp.where(second & three, returned, jnp.where(second & ~two, steps[1:], steps[:1]))
    middle = jnp.where(second & three, steps[:1], steps[1:])
    end = jnp.where(second, steps[1:], returned)
    chosen = jnp.where(slot == 0, lead, jnp.where(slot == 1, middle, end))
    return jnp.where(slot < count, chosen, 0.0), first_step[0]


def solution(mesh):
    split_mesh = Mesh(mesh.devices.reshape(mesh.shape["grp"], 4, 4, 2), GRP_BLK)
    whole = P(GRP_BLK, None)
    placed = (whole,) * 6 + (P(GRP_BLK),) + (P(),) * 6
    return jax.shard_map(
        on_device, mesh=split_mesh, in_specs=placed, out_specs=(whole, P()), check_vma=False
    )
```

time: 192 us -> 159 us (0.83)
  Pallas kernels: 115 us -> 84 us
  local copies, waits for them, and re-layouts: 11.7 us -> 7.1 us
  other arithmetic: 6.19 us -> 8.87 us
    pallas_call x1, Pallas kernels: 77.9 us -> 53.7 us  [on_device(): pl.pallas_call(hours_kernel, out_shape=(jax.ShapeDtypeStruct((HOURS, nb,...]
    pallas_call x1, Pallas kernels: 37 us -> 30.4 us  [on_device(): pl.pallas_call(finish_kernel, out_shape=(jax.ShapeDtypeStruct((1, nb), F3...]
    unnamed x18 -> x15, local copies, waits for them, and re-layouts: 7.09 us -> 3.7 us
    unnamed x0 -> x5, other arithmetic: none -> 3.22 us
where the time goes in v2:
time: 159 us; the launch traced here: 158 us
  Pallas kernels  84 us (53%)
  blocking collectives  44.1 us (28%)
  other arithmetic  8.87 us (6%)
  starting transfers between devices  8.26 us (5%)
  local copies, waits for them, and re-layouts  7.1 us (4%)
  waiting for transfers between devices  3.26 us (2%)
    pallas_call x1, Pallas kernels, on_device(): pl.pallas_call(hours_kernel, out_shape=(jax.ShapeDtypeStruct((HOURS, nb,...  53.7 us
    pallas_call x1, Pallas kernels, on_device(): pl.pallas_call(finish_kernel, out_shape=(jax.ShapeDtypeStruct((1, nb), F3...  30.4 us
    all_to_all x1, blocking collectives, summed_over_all(): piece = lax.all_to_all(pieces, CHIPS, 0, 0, tiled=True).sum(axis=0)  25.8 us
    all_to_all x1, blocking collectives, summed_over_all(): mine = lax.all_to_all(spread, CHIPS, 0, 0, tiled=True).reshape(half, width)  18.3 us
    unnamed x15, local copies, waits for them, and re-layouts  3.7 us
    unnamed x5, other arithmetic  3.22 us
    ppermute x1, starting transfers between devices, on_device(): lax.ppermute(last, GRP_BLK, [(d, d + 1) for d in range(devices - 1)])  3.21 us
  transfers between devices with their start and end apart: 5, of which 2 were waited for; matrix products, arithmetic and copies ran while one was open for 4% of the time, Pallas kernels for 0%

profile of v2, /device:TPU:1, one launch (start us, length us, event | category | flops | bytes accessed | tf_op | source)
XLA Modules:
  0.0 158.4 jit_solution(2143839419935106629)
XLA Ops:
  0.6 0.0 copy-start
  0.6 0.8 convert_element_type.3
  2.1 0.8 constant_dynamic-update-slice_fusion.5
  2.9 0.8 constant_dynamic-update-slice_fusion.4
  3.7 0.8 constant_dynamic-update-slice_fusion.3
  4.5 0.8 constant_dynamic-update-slice_fusion.2
  5.3 0.0 copy-done
  5.3 1.4 fusion.3.state
  6.7 0.0 copy-start.3
  6.8 1.5 collective-permute-start.1
  8.2 3.2 %collective-permute-start = (f32[1,128]{1,0:T(1,128)S(1)}, f32[1,128]{1,0:T(1,128)S(1)}, u32[]{:S(2)}, u32[]{:S(2)}) collective-permute-start(f32[1,128]{1,0:T(1,128)S(1)} %get-tuple-element.22), channel_id=1, source_target_pairs={{0,1},{1,2},{2,3},{3,4},{4,5},{5,6},{6,7},{7,8},{8,9},{9,10},{10,1... | collective-permute-start | bytes 1544 | tf_op jit(solution)/shard_map/ppermute | solution.py:378
  11.5 0.6 pad_add_fusion.place
  12.0 3.1 %copy.15 = f32[768,768]{0,1:T(8,128)} copy(f32[768,768]{1,0:T(8,128)} %border_hbm.3) | data formatting | bytes 4718592 | tf_op args[8]
  15.1 0.0 copy-done.3
  15.1 0.0 collective-permute-done.incoming
  15.1 0.0 copy-start.6
  15.1 0.0 collective-permute-done.1.message
  15.1 0.0 copy-start.2
  15.2 0.5 copy-done.6
  15.6 0.1 copy-done.2
  15.7 53.7 %hours.1 = (f32[2,768,768]{2,1,0:T(8,128)}, f32[3072,128]{1,0:T(8,128)}, f32[2,768]{1,0:T(2,128)}, f32[2,768]{1,0:T(2,128)}) custom-call(s32[2]{0:T(128)} %pad_add_fusion.place, f32[3,1536]{1,0:T(4,128)} %barrier_scale.1, f32[3,768]{1,0:T(4,128)} %regularizer.1, f32[3,768]{1,0:T(4,128)} %availability.1, f32[3,768]{1,0:T(4,128)} %block_rhs.1, ...), custom_call_target="tpu_custom_call" | custom-call | tf_op jit(solution)/shard_map/hours/pallas_call | solution.py:386
  69.4 0.0 copy-start.1
  69.4 2.2 %constant_dynamic-slice_fusion = f32[1536,128]{1,0:T(8,128)} fusion(f32[3072,128]{1,0:T(8,128)} %get-tuple-element.9, s32[]{:T(128)S(6)} %select_n.109), kind=kLoop, calls=%fused_computation.27 | loop fusion | bytes 1572868 | tf_op jit(solution)/shard_map/dynamic_slice | solution.py:351
  71.6 0.0 collective-permute-start.2
  71.6 2.5 %collective-permute-done.2 = f32[1536,128]{1,0:T(8,128)S(1)} collective-permute-done((f32[1536,128]{1,0:T(8,128)}, f32[1536,128]{1,0:T(8,128)S(1)}, u32[]{:S(2)}, u32[]{:S(2)}) %collective-permute-start.2) | collective-permute-done | bytes 786464 | tf_op jit(solution)/shard_map/ppermute | solution.py:352
  74.1 0.0 copy-done.1
  74.1 0.1 dynamic-slice_add_fusion
  74.2 25.8 %all_to_all.10 = f32[64,24,128]{2,1,0:T(8,128)S(1)} all-to-all(f32[64,24,128]{2,1,0:T(8,128)S(1)} %bitcast.13), channel_id=1, replica_groups=mesh['grp'=4,'blk_0'=4,'blk_1'=4,'blk_2'=2] {'grp','blk_0','blk_1'}, dimensions={0} | all-to-all | bytes 1572864 | tf_op jit(solution)/shard_map/all_to_all | solution.py:354
  100.0 0.0 copy-start.4
  100.0 0.0 copy-start.5
  100.0 0.1 reduce_sum.9
  100.1 0.1 broadcast_in_dim.73
  100.2 18.3 %all_to_all.11 = f32[64,24,128]{2,1,0:T(8,128)S(1)} all-to-all(f32[64,24,128]{2,1,0:T(8,128)S(1)} %broadcast_in_dim.73), channel_id=1, replica_groups=mesh['grp'=4,'blk_0'=4,'blk_1'=4,'blk_2'=2] {'grp','blk_0','blk_1'}, dimensions={0} | all-to-all | bytes 1572864 | tf_op jit(solution)/shard_map/all_to_all | solution.py:356
  118.4 3.1 %collective-permute-start.3 = (f32[1536,128]{1,0:T(8,128)S(1)}, f32[1536,128]{1,0:T(8,128)S(1)}, u32[]{:S(2)}, u32[]{:S(2)}) collective-permute-start(f32[1536,128]{1,0:T(8,128)S(1)} %bitcast.14), channel_id=1, source_target_pairs={{0,1},{1,0},{2,3},{3,2},{4,5},{5,4},{6,7},{7,6},{8,9},{9,8},{10,11... | collective-permute-start | bytes 2359304 | tf_op jit(solution)/shard_map/ppermute | solution.py:357
  121.6 0.0 copy-done.4
  121.6 0.6 broadcast_in_dim.74.first_diag
  122.2 0.0 copy-done.5
  122.2 0.6 broadcast_in_dim.75.first_rhs
  122.7 0.8 collective-permute-done.3
  123.5 0.1 broadcast_select_fusion.1
  123.6 1.3 pad_maximum_fusion.packed
  124.8 30.4 %finish.1 = (f32[1,768]{1,0:T(1,128)}, f32[2,768]{1,0:T(2,128)}, f32[1,768]{1,0:T(1,128)}) custom-call(s32[2]{0:T(128)} %pad_add_fusion.place, f32[3072,128]{1,0:T(8,128)} %pad_maximum_fusion.packed, f32[1,768]{1,0:T(1,128)} %broadcast_in_dim.74.first_diag, f32[1,768]{1,0:T(1,128)} %broadcast_in_dim.75.first_rhs, f32[2,768]{1,0:T(2,128)} %get-tuple-element.10.avail, ...), custom_call_target="tpu_custom_call" | custom-call | tf_op jit(solution)/shard_map/finish/pallas_call | solution.py:406
  155.2 0.5 collective-permute-start.4
  155.7 1.3 reduce.3
  157.0 0.0 collective-permute-done.4
  157.0 0.8 fusion
  157.8 0.7 select_select_fusion
  (4 shorter events, 0.0 us)
Async XLA Ops:
  0.6 4.7 %copy-start = (f32[128,1536]{1,0:T(8,128)S(1)}, f32[128,1536]{1,0:T(8,128)}, u32[]{:S(2)}) copy-start(f32[128,1536]{1,0:T(8,128)} %param.22) | copy-start | bytes 2359300
  6.7 8.4 %copy-start.3 = (f32[3,128]{1,0:T(4,128)}, f32[3,128]{1,0:T(4,128)S(1)}, u32[]{:S(2)}) copy-start(f32[3,128]{1,0:T(4,128)S(1)} %fusion.3.state) | copy-start | bytes 4612
  6.8 8.4 %collective-permute-start.1 = (f32[1,4096]{1,0:T(1,128)S(1)}, f32[1,4096]{1,0:T(1,128)S(1)}, u32[]{:S(2)}, u32[]{:S(2)}) collective-permute-start(f32[1,4096]{1,0:T(1,128)S(1)} %get-tuple-element.21), channel_id=1, source_target_pairs={{0,1},{1,0},{2,3},{3,2},{4,5},{5,4},{6,7},{7,6},{8,9},{9,8},{10,11... | collective-permute-start | bytes 49160 | tf_op jit(solution)/shard_map/ppermute | solution.py:381
  8.2 6.9 %collective-permute-start = (f32[1,128]{1,0:T(1,128)S(1)}, f32[1,128]{1,0:T(1,128)S(1)}, u32[]{:S(2)}, u32[]{:S(2)}) collective-permute-start(f32[1,128]{1,0:T(1,128)S(1)} %get-tuple-element.22), channel_id=1, source_target_pairs={{0,1},{1,2},{2,3},{3,4},{4,5},{5,6},{6,7},{7,8},{8,9},{9,10},{10,1... | collective-permute-start | bytes 1544 | tf_op jit(solution)/shard_map/ppermute | solution.py:378
  15.1 0.5 copy-start.6
  15.1 0.6 copy-start.2
  69.4 4.7 %copy-start.1 = (f32[3072,128]{1,0:T(8,128)S(1)}, f32[3072,128]{1,0:T(8,128)}, u32[]{:S(2)}) copy-start(f32[3072,128]{1,0:T(8,128)} %get-tuple-element.9) | copy-start | bytes 4718596
  71.6 2.5 %collective-permute-start.2 = (f32[1536,128]{1,0:T(8,128)}, f32[1536,128]{1,0:T(8,128)S(1)}, u32[]{:S(2)}, u32[]{:S(2)}) collective-permute-start(f32[1536,128]{1,0:T(8,128)} %constant_dynamic-slice_fusion), channel_id=1, source_target_pairs={{0,1},{1,0},{2,3},{3,2},{4,5},{5,4},{6,7},{7,6},{8,9},{9,8},{10,11... | collective-permute-start | bytes 2359304 | tf_op jit(solution)/shard_map/ppermute | solution.py:352
  100.0 21.6 %copy-start.4 = (f32[768]{0:T(1024)S(1)}, f32[768]{0:T(1024)}, u32[]{:S(2)}) copy-start(f32[768]{0:T(1024)} %param.24) | copy-start | bytes 9220
  100.0 22.1 %copy-start.5 = (f32[768]{0:T(1024)S(1)}, f32[768]{0:T(1024)}, u32[]{:S(2)}) copy-start(f32[768]{0:T(1024)} %param.25) | copy-start | bytes 9220
  118.4 5.0 %collective-permute-start.3 = (f32[1536,128]{1,0:T(8,128)S(1)}, f32[1536,128]{1,0:T(8,128)S(1)}, u32[]{:S(2)}, u32[]{:S(2)}) collective-permute-start(f32[1536,128]{1,0:T(8,128)S(1)} %bitcast.14), channel_id=1, source_target_pairs={{0,1},{1,0},{2,3},{3,2},{4,5},{5,4},{6,7},{7,6},{8,9},{9,8},{10,11... | collective-permute-start | bytes 2359304 | tf_op jit(solution)/shard_map/ppermute | solution.py:357
  155.2 1.7 %collective-permute-start.4 = (f32[1,768]{1,0:T(1,128)}, f32[1,768]{1,0:T(1,128)S(1)}, u32[]{:S(2)}, u32[]{:S(2)}) collective-permute-start(f32[1,768]{1,0:T(1,128)} %get-tuple-element.13), channel_id=1, source_target_pairs={{0,1},{1,0},{2,3},{3,2},{4,5},{5,4},{6,7},{7,6},{8,9},{9,8},{10,11... | collective-permute-start | bytes 9224 | tf_op jit(solution)/shard_map/ppermute | solution.py:418

commit v3 on v2

--- a/solution.py
+++ b/solution.py
@@ -131,7 +131,7 @@
     )
 
 
-def sweep_inverse(mats, tiles, columns, rows, reach, woven):
+def sweep_inverse(mats, tiles, columns, rows, reach):
     count, n, _ = mats.shape
     each = range(count)
     last = n // TILE - 1
@@ -161,10 +161,7 @@
         after = pl.ds(pl.multiple_of((k + 1) * TILE, TILE), TILE)
         for m in each:
             tiles[m][...] = mats[m, after, after] - mm(columns[m, after, :], rows[m, :, after])
-        invert_tiles([tiles[m] for m in each], reach, work if woven else ())
-        if not woven:
-            for item in work:
-                item()
+        invert_tiles([tiles[m] for m in each], reach, work)
         return carry
 
     for m in each:
@@ -197,7 +194,7 @@
 def hours_kernel(
     place, barrier_scale, regularizer, availability, block_rhs, link_mask, state, incoming, message,
     link_in, constraints, border_hbm, border_t_hbm,
-    inverses_hbm, packed, solved, avail,
+    inverses_hbm, kept, lent, solved, avail,
     inverses, border, border_t, scaled, coupled, columns, rows, sems, *tiles,
 ):
     nb, nv = constraints.shape
@@ -226,17 +223,20 @@
     for m in range(HOURS):
         scaled[...] = (constraints[...].astype(F32) * scale[m]).astype(BF16)
         for c in range(0, nb, CHUNK):
-            both = lax.dot_general(
+            inverses[m, :, c : c + CHUNK] = lax.dot_general(
                 scaled[...], constraints[c : c + CHUNK, :], NT, preferred_element_type=F32
-            ) + lax.dot_general(
-                constraints[...], scaled[c : c + CHUNK, :], NT, preferred_element_type=F32
             )
-            inverses[m, :, c : c + CHUNK] = 0.5 * both
-        for c in range(0, nb, TILE):
-            block = inverses[m, c : c + TILE, c : c + TILE]
-            extra = jnp.where(eye, diag[m][:, c : c + TILE], 0.0)
-            inverses[m, c : c + TILE, c : c + TILE] = block + extra
-    sweep_inverse(inverses, tiles, columns, rows, 64, True)
+        for i in range(0, nb, TILE):
+            down = slice(i, i + TILE)
+            for j in range(0, i, TILE):
+                across = slice(j, j + TILE)
+                block = 0.5 * (inverses[m, down, across] + inverses[m, across, down].T)
+                inverses[m, down, across] = block
+                inverses[m, across, down] = block.T
+            block = inverses[m, down, down]
+            extra = jnp.where(eye, diag[m][:, down], 0.0)
+            inverses[m, down, down] = 0.5 * (block + block.T) + extra
+    sweep_inverse(inverses, tiles, columns, rows, 64)
     store = pltpu.make_async_copy(inverses, inverses_hbm, sems.at[2])
     store.start()
     own_state = [state[s : s + 1, :] for s in range(3)]
@@ -267,24 +267,45 @@
         load.wait()
     gradient = jnp.sum(as_column(total) * border[...], axis=0, keepdims=True)
     coupled[...] = dot3_nt(middle, border_t[...])
+    half = kept.shape[0]
+
+    def put(row, value):
+        first = (row < half) == (place[1] == 0)
+        at = slice(row % half, row % half + value.shape[0])
+
+        @pl.when(first)
+        def _():
+            kept[at, :] = value
+
+        @pl.when(jnp.logical_not(first))
+        def _():
+            lent[at, :] = value
+
     row = 0
     for i in range(0, nb, TILE):
         part = dot3(border_t[i : i + TILE, :], coupled[:, : i + TILE])
         for j in range(0, i + TILE, TILE):
-            packed[row : row + TILE, :] = part[:, j : j + TILE]
+            put(row, part[:, j : j + TILE])
             row += TILE
-    packed[row:, :] = jnp.zeros((packed.shape[0] - row, TILE), F32)
-    for t in range(nb // TILE):
-        packed[row + t : row + t + 1, :] = gradient[:, t * TILE : (t + 1) * TILE]
+    parts = [gradient[:, t * TILE : (t + 1) * TILE] for t in range(nb // TILE)]
+    parts.append(jnp.zeros((2 * half - row - len(parts), TILE), F32))
+    put(row, jnp.concatenate(parts, axis=0))
     store.wait()
 
 
+def as_row(column):
+    wide = jnp.broadcast_to(column, (TILE, TILE))
+    return jnp.sum(jnp.where(diagonal(), wide, 0.0), axis=0, keepdims=True)
+
+
 def finish_kernel(
-    place, packed, first_diag, first_rhs, avail, solved, border_hbm, inverses_hbm,
+    place, mine, other, first_diag, first_rhs, avail, solved, border_hbm, inverses_hbm,
     first_step, steps, sent,
-    schur, border, inverses, columns, rows, sems, *tiles,
+    schur, rhs, heads, border, inverses, sems, tile,
 ):
-    nb = schur.shape[1]
+    nb = schur.shape[0]
+    count = nb // TILE
+    half = mine.shape[0]
     loads = [
         pltpu.make_async_copy(border_hbm, border, sems.at[0]),
         pltpu.make_async_copy(inverses_hbm, inverses, sems.at[1]),
@@ -292,32 +313,88 @@
     for load in loads:
         load.start()
     eye = diagonal()
+
+    def get(row, rows):
+        at = slice(row % half, row % half + rows)
+        return jnp.where((row < half) == (place[1] == 0), mine[at, :], other[at, :])
+
     row = 0
     for i in range(0, nb, TILE):
         for j in range(0, i + TILE, TILE):
-            block = packed[row : row + TILE, :]
+            block = get(row, TILE)
             row += TILE
             if i == j:
                 block = block + jnp.where(eye, first_diag[:, i : i + TILE], 0.0)
-            else:
-                schur[0, j : j + TILE, i : i + TILE] = block.T
-            schur[0, i : i + TILE, j : j + TILE] = block
-    sweep_inverse(schur, tiles, columns, rows, TILE, False)
-    gradient = jnp.concatenate(
-        [packed[row + t : row + t + 1, :] for t in range(nb // TILE)], axis=1
-    )
-    rhs = as_column(gradient - first_rhs[...])
-    x = jnp.sum(rhs * schur[0], axis=0, keepdims=True)
-    first_step[...] = x
+            schur[i : i + TILE, j : j + TILE] = block
+    tail = get(row, 8)
+    gradient = jnp.concatenate([tail[t : t + 1, :] for t in range(count)], axis=1)
+    rhs[...] = as_column(gradient - first_rhs[...])
+
+    def eliminate(k):
+        here, below = slice(k * TILE, (k + 1) * TILE), slice((k + 1) * TILE, nb)
+        pivot = tile[...]
+        column = schur[below, here]
+        scaled = dot3(column, pivot)
+        factor = left(scaled)
+        h, l = split(column)
+        across = jnp.concatenate([h, l, h], 1)
+        for c in range(0, nb - (k + 1) * TILE, TILE):
+            start = (k + 1) * TILE + c
+            at = (slice(start, nb), slice(start, start + TILE))
+            schur[at] = schur[at] - lax.dot_general(
+                factor[c:, :], across[c : c + TILE, :], NT, preferred_element_type=F32
+            )
+        schur[below, here] = scaled
+        own = rhs[here, :]
+        heads[k : k + 1, :] = jnp.sum(own * pivot, axis=0, keepdims=True)
+        rhs[below, :] = rhs[below, :] - jnp.sum(scaled * as_row(own), axis=1, keepdims=True)
+
+    def step(k, carry):
+        for done in range(1, count):
+            pl.when(k == done)(functools.partial(eliminate, done - 1))
+        here = pl.ds(pl.multiple_of(k * TILE, TILE), TILE)
+        tile[...] = schur[here, here]
+        invert_tiles([tile], TILE)
+        return carry
+
+    lax.fori_loop(0, count, step, 0)
+    x = jnp.sum(rhs[nb - TILE :, :] * tile[...], axis=0, keepdims=True)
+    found_row, found_column = x, as_column(x)
+    for k in range(count - 2, -1, -1):
+        below = schur[(k + 1) * TILE :, k * TILE : (k + 1) * TILE]
+        x = heads[k : k + 1, :] - jnp.sum(found_column * below, axis=0, keepdims=True)
+        found_row = jnp.concatenate([x, found_row], axis=1)
+        found_column = jnp.concatenate([as_column(x), found_column], axis=0)
+    first_step[...] = found_row
     for load in loads:
         load.wait()
-    v = jnp.sum(border[...] * x, axis=1, keepdims=True)
+    v = jnp.sum(border[...] * found_row, axis=1, keepdims=True)
     for m in range(HOURS):
         w = as_column(avail[m : m + 1, :]) * v
         steps[m : m + 1, :] = solved[m : m + 1, :] - jnp.sum(
             w * inverses[m], axis=0, keepdims=True
         )
     sent[...] = jnp.where(place[1] == 1, steps[0:1, :], steps[1:2, :])
+
+
+def message_kernel(
+    place, barrier_scale, regularizer, availability, block_rhs, link_mask, primal, link_out,
+    state, last, message,
+):
+    padded = jnp.concatenate([primal[...], jnp.zeros((5, primal.shape[1]), F32)], axis=0)
+    states = dot3_nt(padded, link_out[...])
+    state[...] = states[:3, :]
+    count, second = place[0], place[1] == 1
+    last[...] = jnp.where(
+        count == 3, states[2:3, :], jnp.where(count == 2, states[1:2, :], states[:1, :])
+    )
+    at = 0
+    for field in (barrier_scale, regularizer, availability, block_rhs, link_mask):
+        width = field.shape[1]
+        lent = jnp.where(second, field[0:1, :], field[2:3, :])
+        message[:, at : at + width] = lent.astype(F32)
+        at += width
+    message[:, at:] = states[1:2, :]
 
 
 PARAMS = pltpu.CompilerParams(vmem_limit_bytes=56 * 2**20)
@@ -341,22 +418,13 @@
     ]
 
 
-def summed_over_all(array):
+def summed_over_chips(array):
     rows, width = array.shape
-    half = rows // 2
-    core = lax.axis_index(CORE)
     chips = lax.axis_size(CHIPS)
-    pair = [(0, 1), (1, 0)]
-    kept = lax.dynamic_slice_in_dim(array, core * half, half, 0)
-    sent = lax.dynamic_slice_in_dim(array, (1 - core) * half, half, 0)
-    mine = kept + lax.ppermute(sent, CORE, pair)
-    pieces = mine.reshape(chips, half // chips, width)
+    pieces = array.reshape(chips, rows // chips, width)
     piece = lax.all_to_all(pieces, CHIPS, 0, 0, tiled=True).sum(axis=0)
     spread = jnp.broadcast_to(piece[None], (chips, *piece.shape))
-    mine = lax.all_to_all(spread, CHIPS, 0, 0, tiled=True).reshape(half, width)
-    other = lax.ppermute(mine, CORE, pair)
-    first = core == 0
-    return jnp.concatenate([jnp.where(first, mine, other), jnp.where(first, other, mine)], axis=0)
+    return lax.all_to_all(spread, CHIPS, 0, 0, tiled=True).reshape(rows, width)
 
 
 def on_device(
@@ -370,29 +438,36 @@
     devices = lax.axis_size(GRP_BLK)
     pair = [(0, 1), (1, 0)]
     place = jnp.stack([count, core])
-    state = lax.dot_general(
-        primal, link_out, NT, precision=HIGHEST, preferred_element_type=F32
-    )
-    two, three = count >= 2, count == 3
-    last = jnp.where(three, state[2:], jnp.where(two, state[1:2], state[:1]))
+    three, two = count == 3, count >= 2
+    nk = link_in.shape[1]
+    state, last, lent = pl.pallas_call(
+        message_kernel,
+        out_shape=(
+            jax.ShapeDtypeStruct((3, nk), F32),
+            jax.ShapeDtypeStruct((1, nk), F32),
+            jax.ShapeDtypeStruct((1, nv + 3 * nb + 2 * nk), F32),
+        ),
+        in_specs=spaces(8, (0,), ()),
+        compiler_params=PARAMS,
+        name="message",
+    )(place, barrier_scale, regularizer, availability, block_rhs, link_mask, primal, link_out)
     incoming = lax.ppermute(last, GRP_BLK, [(d, d + 1) for d in range(devices - 1)])
-    fields = (barrier_scale, regularizer, availability, block_rhs, link_mask.astype(F32))
-    lent = [jnp.where(second, field[:1], field[2:]) for field in fields]
-    message = lax.ppermute(jnp.concatenate([*lent, state[1:2]], axis=1), CORE, pair)
+    message = lax.ppermute(lent, CORE, pair)
     packed_rows = (nb // TILE) * (nb // TILE + 1) // 2 * TILE + 8
     packed_rows = -(-packed_rows // (devices * 8)) * devices * 8
     square = pltpu.VMEM((nb, nb), F32)
     pairs = pltpu.VMEM((HOURS, nb, nb), F32)
-    inverses, packed, solved, avail = pl.pallas_call(
+    inverses, kept, sent, solved, avail = pl.pallas_call(
         hours_kernel,
         out_shape=(
             jax.ShapeDtypeStruct((HOURS, nb, nb), F32),
-            jax.ShapeDtypeStruct((packed_rows, TILE), F32),
+            jax.ShapeDtypeStruct((packed_rows // 2, TILE), F32),
+            jax.ShapeDtypeStruct((packed_rows // 2, TILE), F32),
             jax.ShapeDtypeStruct((HOURS, nb), F32),
             jax.ShapeDtypeStruct((HOURS, nb), F32),
         ),
         in_specs=spaces(13, (0,), (11, 12)),
-        out_specs=spaces(4, (), (0,)),
+        out_specs=spaces(5, (), (0,)),
         scratch_shapes=[
             pairs, square, square, pltpu.VMEM((nb, nv), BF16), square, *sweep_scratch(HOURS, nb)
         ],
@@ -402,7 +477,8 @@
         place, barrier_scale, regularizer, availability, block_rhs, link_mask, state, incoming,
         message, link_in, constraints, border, border.T,
     )
-    total = summed_over_all(packed)
+    mine = summed_over_chips(kept + lax.ppermute(sent, CORE, pair))
+    other = lax.ppermute(mine, CORE, pair)
     first_step, steps, sent = pl.pallas_call(
         finish_kernel,
         out_shape=(
@@ -410,11 +486,14 @@
             jax.ShapeDtypeStruct((HOURS, nb), F32),
             jax.ShapeDtypeStruct((1, nb), F32),
         ),
-        in_specs=spaces(8, (0,), (6, 7)),
-        scratch_shapes=[pltpu.VMEM((1, nb, nb), F32), square, pairs, *sweep_scratch(1, nb)],
+        in_specs=spaces(9, (0,), (7, 8)),
+        scratch_shapes=[
+            square, pltpu.VMEM((nb, 1), F32), pltpu.VMEM((8, TILE), F32), square, pairs,
+            pltpu.SemaphoreType.DMA((2,)), pltpu.VMEM((TILE, TILE), F32),
+        ],
         compiler_params=PARAMS,
         name="finish",
-    )(place, total, first_diag[None], first_rhs[None], avail, solved, border, inverses)
+    )(place, mine, other, first_diag[None], first_rhs[None], avail, solved, border, inverses)
     returned = lax.ppermute(sent, CORE, pair)
     slot = jnp.arange(3, dtype=jnp.int32)[:, None]
     lead = jnp.where(second & three, returned, jnp.where(second & ~two, steps[1:], steps[:1]))

time: 159 us -> 154 us (0.969)
  other arithmetic: 8.87 us -> 4.71 us
  Pallas kernels: 84 us -> 86.1 us
    unnamed x5 -> x0, other arithmetic: 3.22 us -> none
    pallas_call x0 -> x1, Pallas kernels: none -> 2.28 us  [on_device(): pl.pallas_call(message_kernel, out_shape=(jax.ShapeDtypeStruct((3, nk), F...]
    dynamic_slice x1 -> x0, local copies, waits for them, and re-layouts: 2.2 us -> none  [summed_over_all(): sent = lax.dynamic_slice_in_dim(array, (1 - core) * half, half, 0)]
    unnamed x15 -> x13, local copies, waits for them, and re-layouts: 3.7 us -> 4.62 us
where the time goes in v3:
time: 154 us
  Pallas kernels  86.1 us (56%)
  blocking collectives  44.1 us (29%)
  starting transfers between devices  8.25 us (5%)
  local copies, waits for them, and re-layouts  5.84 us (4%)
  other arithmetic  4.71 us (3%)
  waiting for transfers between devices  3.22 us (2%)
    pallas_call x1, Pallas kernels, on_device(): pl.pallas_call(hours_kernel, out_shape=(jax.ShapeDtypeStruct((HOURS, nb,...  54.6 us
    pallas_call x1, Pallas kernels, on_device(): pl.pallas_call(finish_kernel, out_shape=(jax.ShapeDtypeStruct((1, nb), F3...  29.2 us
    all_to_all x1, blocking collectives, summed_over_chips(): piece = lax.all_to_all(pieces, CHIPS, 0, 0, tiled=True).sum(axis=0)  25.8 us
    all_to_all x1, blocking collectives, summed_over_chips(): return lax.all_to_all(spread, CHIPS, 0, 0, tiled=True).reshape(rows, width)  18.3 us
    unnamed x13, local copies, waits for them, and re-layouts  4.62 us
    ppermute x1, starting transfers between devices, on_device(): lax.ppermute(last, GRP_BLK, [(d, d + 1) for d in range(devices - 1)])  3.19 us
    ppermute x1, starting transfers between devices, on_device(): other = lax.ppermute(mine, CORE, pair)  3.13 us
  transfers between devices with their start and end apart: 5, of which 2 were waited for; matrix products, arithmetic and copies ran while one was open for 4% of the time, Pallas kernels for 0%

profile of v3, /device:TPU:1, one launch (start us, length us, event | category | flops | bytes accessed | tf_op | source)
XLA Modules:
  0.0 153.5 jit_solution(16819177040942498235)
XLA Ops:
  1.3 0.7 pad_add_fusion.place
  1.9 2.3 %message.1 = (f32[3,128]{1,0:T(4,128)}, f32[1,128]{1,0:T(1,128)}, f32[1,4096]{1,0:T(1,128)}) custom-call(s32[2]{0:T(128)} %pad_add_fusion.place, f32[3,1536]{1,0:T(4,128)} %barrier_scale.3, f32[3,768]{1,0:T(4,128)} %regularizer.3, f32[3,768]{1,0:T(4,128)} %availability.3, f32[3,768]{1,0:T(4,128)} %block_rhs.3, s32[3,128]{1,0:T(4,128)} %link_mask.3, ...), custom_call_target="tpu_custom_call" | custom-call | tf_op jit(solution)/shard_map/message/pallas_call | solution.py:443
  4.2 1.4 collective-permute-start.1
  5.6 3.2 %collective-permute-start = (f32[1,128]{1,0:T(1,128)}, f32[1,128]{1,0:T(1,128)S(1)}, u32[]{:S(2)}, u32[]{:S(2)}) collective-permute-start(f32[1,128]{1,0:T(1,128)} %get-tuple-element.14), channel_id=1, source_target_pairs={{0,1},{1,2},{2,3},{3,4},{4,5},{5,6},{6,7},{7,8},{8,9},{9,10},{10,1... | collective-permute-start | bytes 1544 | tf_op jit(solution)/shard_map/ppermute | solution.py:454
  8.8 3.1 %copy.15 = f32[768,768]{0,1:T(8,128)} copy(f32[768,768]{1,0:T(8,128)} %border_hbm.3) | data formatting | bytes 4718592 | tf_op args[8]
  11.9 0.0 collective-permute-done.incoming
  11.9 0.0 copy-start.5
  11.9 0.0 collective-permute-done.1.message
  11.9 0.0 copy-start.2
  11.9 0.5 copy-done.5
  12.4 0.1 copy-done.2
  12.5 54.6 %hours.1 = (f32[2,768,768]{2,1,0:T(8,128)}, f32[1536,128]{1,0:T(8,128)}, f32[1536,128]{1,0:T(8,128)}, f32[2,768]{1,0:T(2,128)}, f32[2,768]{1,0:T(2,128)}) custom-call(s32[2]{0:T(128)} %pad_add_fusion.place, f32[3,1536]{1,0:T(4,128)} %barrier_scale.3, f32[3,768]{1,0:T(4,128)} %regularizer.3, f32[3,768]{1,0:T(4,128)} %availability.3, f32[3,768]{1,0:T(4,128)} %block_rhs.3, ...), custom_call_target="tpu_custom_call" | custom-call | tf_op jit(solution)/shard_map/hours/pallas_call | solution.py:460
  67.1 0.1 collective-permute-start.2
  67.2 2.5 %collective-permute-done.2 = f32[1536,128]{1,0:T(8,128)S(1)} collective-permute-done((f32[1536,128]{1,0:T(8,128)}, f32[1536,128]{1,0:T(8,128)S(1)}, u32[]{:S(2)}, u32[]{:S(2)}) %collective-permute-start.2) | collective-permute-done | bytes 786464 | tf_op jit(solution)/shard_map/ppermute | solution.py:480
  69.7 1.2 add.3
  70.9 0.0 copy-start.3
  70.9 0.0 copy-start.4
  70.9 25.8 %all_to_all.10 = f32[64,24,128]{2,1,0:T(8,128)S(1)} all-to-all(f32[64,24,128]{2,1,0:T(8,128)S(1)} %bitcast.11), channel_id=1, replica_groups=mesh['grp'=4,'blk_0'=4,'blk_1'=4,'blk_2'=2] {'grp','blk_0','blk_1'}, dimensions={0} | all-to-all | bytes 1572864 | tf_op jit(solution)/shard_map/all_to_all | solution.py:425
  96.7 0.1 reduce_sum.9
  96.8 0.1 broadcast_in_dim.73
  96.9 18.3 %all_to_all.11 = f32[64,24,128]{2,1,0:T(8,128)S(1)} all-to-all(f32[64,24,128]{2,1,0:T(8,128)S(1)} %broadcast_in_dim.73), channel_id=1, replica_groups=mesh['grp'=4,'blk_0'=4,'blk_1'=4,'blk_2'=2] {'grp','blk_0','blk_1'}, dimensions={0} | all-to-all | bytes 1572864 | tf_op jit(solution)/shard_map/all_to_all | solution.py:427
  115.1 0.0 copy-start
  115.1 3.1 %collective-permute-start.3 = (f32[1536,128]{1,0:T(8,128)S(1)}, f32[1536,128]{1,0:T(8,128)S(1)}, u32[]{:S(2)}, u32[]{:S(2)}) collective-permute-start(f32[1536,128]{1,0:T(8,128)S(1)} %bitcast.9), channel_id=1, source_target_pairs={{0,1},{1,0},{2,3},{3,2},{4,5},{5,4},{6,7},{7,6},{8,9},{9,8},{10,11... | collective-permute-start | bytes 2359304 | tf_op jit(solution)/shard_map/ppermute | solution.py:481
  118.3 0.0 copy-done.3
  118.3 0.6 broadcast_in_dim.74.first_diag
  118.8 0.0 copy-done.4
  118.8 0.6 broadcast_in_dim.75.first_rhs
  119.4 0.7 collective-permute-done.3.other
  120.2 0.0 copy-start.1
  120.2 0.0 copy-done
  120.2 0.9 copy-done.1
  121.1 29.2 %finish.1 = (f32[1,768]{1,0:T(1,128)}, f32[2,768]{1,0:T(2,128)}, f32[1,768]{1,0:T(1,128)}) custom-call(s32[2]{0:T(128)} %pad_add_fusion.place, f32[1536,128]{1,0:T(8,128)} %bitcast.10, f32[1536,128]{1,0:T(8,128)} %copy-done.1, f32[1,768]{1,0:T(1,128)} %broadcast_in_dim.74.first_diag, f32[1,768]{1,0:T(1,128)} %broadcast_in_dim.75.first_rhs, ...), custom_call_target="tpu_custom_call" | custom-call | tf_op jit(solution)/shard_map/finish/pallas_call | solution.py:482
  150.3 0.5 collective-permute-start.4
  150.8 1.3 reduce.3
  152.1 0.0 collective-permute-done.4
  152.1 0.8 fusion
  152.9 0.7 select_select_fusion
  (2 shorter events, 0.0 us)
Async XLA Ops:
  4.2 7.7 %collective-permute-start.1 = (f32[1,4096]{1,0:T(1,128)}, f32[1,4096]{1,0:T(1,128)S(1)}, u32[]{:S(2)}, u32[]{:S(2)}) collective-permute-start(f32[1,4096]{1,0:T(1,128)} %get-tuple-element.15), channel_id=1, source_target_pairs={{0,1},{1,0},{2,3},{3,2},{4,5},{5,4},{6,7},{7,6},{8,9},{9,8},{10,11... | collective-permute-start | bytes 49160 | tf_op jit(solution)/shard_map/ppermute | solution.py:455
  5.6 6.3 %collective-permute-start = (f32[1,128]{1,0:T(1,128)}, f32[1,128]{1,0:T(1,128)S(1)}, u32[]{:S(2)}, u32[]{:S(2)}) collective-permute-start(f32[1,128]{1,0:T(1,128)} %get-tuple-element.14), channel_id=1, source_target_pairs={{0,1},{1,2},{2,3},{3,4},{4,5},{5,6},{6,7},{7,8},{8,9},{9,10},{10,1... | collective-permute-start | bytes 1544 | tf_op jit(solution)/shard_map/ppermute | solution.py:454
  11.9 0.5 copy-start.5
  11.9 0.6 copy-start.2
  67.1 2.6 %collective-permute-start.2 = (f32[1536,128]{1,0:T(8,128)}, f32[1536,128]{1,0:T(8,128)S(1)}, u32[]{:S(2)}, u32[]{:S(2)}) collective-permute-start(f32[1536,128]{1,0:T(8,128)} %get-tuple-element.17), channel_id=1, source_target_pairs={{0,1},{1,0},{2,3},{3,2},{4,5},{5,4},{6,7},{7,6},{8,9},{9,8},{10,11... | collective-permute-start | bytes 2359304 | tf_op jit(solution)/shard_map/ppermute | solution.py:480
  70.9 47.4 %copy-start.3 = (f32[768]{0:T(1024)S(1)}, f32[768]{0:T(1024)}, u32[]{:S(2)}) copy-start(f32[768]{0:T(1024)} %param.24) | copy-start | bytes 9220
  70.9 48.0 %copy-start.4 = (f32[768]{0:T(1024)S(1)}, f32[768]{0:T(1024)}, u32[]{:S(2)}) copy-start(f32[768]{0:T(1024)} %param.25) | copy-start | bytes 9220
  115.1 5.1 %copy-start = (f32[64,24,128]{2,1,0:T(8,128)}, f32[64,24,128]{2,1,0:T(8,128)S(1)}, u32[]{:S(2)}) copy-start(f32[64,24,128]{2,1,0:T(8,128)S(1)} %all_to_all.11) | copy-start | bytes 2359300
  115.1 5.0 %collective-permute-start.3 = (f32[1536,128]{1,0:T(8,128)S(1)}, f32[1536,128]{1,0:T(8,128)S(1)}, u32[]{:S(2)}, u32[]{:S(2)}) collective-permute-start(f32[1536,128]{1,0:T(8,128)S(1)} %bitcast.9), channel_id=1, source_target_pairs={{0,1},{1,0},{2,3},{3,2},{4,5},{5,4},{6,7},{7,6},{8,9},{9,8},{10,11... | collective-permute-start | bytes 2359304 | tf_op jit(solution)/shard_map/ppermute | solution.py:481
  120.2 0.9 copy-start.1
  150.3 1.7 %collective-permute-start.4 = (f32[1,768]{1,0:T(1,128)}, f32[1,768]{1,0:T(1,128)S(1)}, u32[]{:S(2)}, u32[]{:S(2)}) collective-permute-start(f32[1,768]{1,0:T(1,128)} %get-tuple-element.21), channel_id=1, source_target_pairs={{0,1},{1,0},{2,3},{3,2},{4,5},{5,4},{6,7},{7,6},{8,9},{9,8},{10,11... | collective-permute-start | bytes 9224 | tf_op jit(solution)/shard_map/ppermute | solution.py:497

commit v4 on v3

--- a/solution.py
+++ b/solution.py
@@ -29,23 +29,21 @@
     return jnp.broadcast_to(x[j : j + 1, :], x.shape)
 
 
-def invert_tiles(refs, reach, work=()):
+def invert_tiles(refs, window, work=()):
     work = list(work)
     done = 0
     shape = (PANEL, TILE)
     lane = lax.broadcasted_iota(jnp.int32, shape, 1)
     sub = lax.broadcasted_iota(jnp.int32, shape, 0)
     panels = TILE // PANEL
-    groups = reach // PANEL
+    groups = window // PANEL
+    windows = TILE // window
     each = range(len(refs))
-    for base in range(0, TILE, reach):
-        parts = [
-            [ref[base + PANEL * g : base + PANEL * (g + 1), :] for g in range(groups)]
-            for ref in refs
-        ]
-        before = [ref[...] for ref in refs] if reach < TILE else None
-        for t in range(groups):
-            lo = base + PANEL * t
+    parts = [[ref[PANEL * g : PANEL * (g + 1), :] for g in range(panels)] for ref in refs]
+    for w in range(windows):
+        near = range(groups * w, min(groups * (w + 2), panels))
+        for t in range(groups * w, groups * (w + 1)):
+            lo = PANEL * t
             inside = (lane >= lo) & (lane < lo + PANEL)
             eye = lane == sub + lo
             rows = [parts[m][t] for m in each]
@@ -61,7 +59,7 @@
                         c = row_of(cols[m][q], j) * inverse[m]
                         cols[m][q] = jnp.where(own, c, cols[m][q] - col[m] * c)
                 rows = [jnp.where(own, pivot[m], rows[m] - col[m] * pivot[m]) for m in each]
-            others = [(t + s) % groups for s in range(1, groups)]
+            others = [i for i in near if i > t] + [i for i in near if i < t]
             for m in each:
                 spread = [row_of(rows[m], j) for j in range(PANEL)]
                 acc = {i: jnp.where(inside, 0.0, parts[m][i]) for i in others}
@@ -74,31 +72,33 @@
                 for i in others:
                     parts[m][i] = acc[i]
                 parts[m][t] = rows[m]
-            past = lo // PANEL + 1
+            past = t + 1
             while done < len(work) and done * panels < past * len(work):
                 work[done]()
                 done += 1
-        if reach == TILE:
-            for m in each:
-                for g in range(groups):
-                    refs[m][PANEL * g : PANEL * (g + 1), :] = parts[m][g]
+        far = [i for i in range(panels) if i not in near]
+        if not far:
             continue
-        wide = lax.broadcasted_iota(jnp.int32, (TILE, TILE), 1)
-        tall = lax.broadcasted_iota(jnp.int32, (TILE, TILE), 0)
-        own_lanes = (wide >= base) & (wide < base + reach)
-        own_rows = (tall >= base) & (tall < base + reach)
+        base = window * w
+        wide = lax.broadcasted_iota(jnp.int32, (PANEL * len(far), TILE), 1)
+        own_lanes = (wide >= base) & (wide < base + window)
         for m in each:
-            block = list(parts[m])
-            if base:
-                block.insert(0, jnp.zeros((base, TILE), F32))
-            if base + reach < TILE:
-                block.append(jnp.zeros((TILE - base - reach, TILE), F32))
-            block = jnp.concatenate(block, axis=0)
-            bh, bl = split(block)
-            xh, xl = split(before[m])
+            block = parts[m][groups * w : groups * (w + 1)]
+            above, under = base, TILE - base - window
+            if above:
+                block = [jnp.zeros((above, TILE), F32), *block]
+            if under:
+                block = [*block, jnp.zeros((under, TILE), F32)]
+            bh, bl = split(jnp.concatenate(block, axis=0))
+            old = jnp.concatenate([parts[m][i] for i in far], axis=0)
+            xh, xl = split(old)
             change = mm(jnp.concatenate([xh, xl], 1), jnp.concatenate([bh, bh], 0)) + mm(xh, bl)
-            rest = jnp.where(own_lanes, 0.0, before[m]) - change
-            refs[m][...] = jnp.where(own_rows, block, rest)
+            new = jnp.where(own_lanes, 0.0, old) - change
+            for s, i in enumerate(far):
+                parts[m][i] = new[PANEL * s : PANEL * (s + 1), :]
+    for m in each:
+        for g in range(panels):
+            refs[m][PANEL * g : PANEL * (g + 1), :] = parts[m][g]
 
 
 def mm(a, b):
@@ -131,24 +131,24 @@
     )
 
 
-def sweep_inverse(mats, tiles, columns, rows, reach):
+def sweep_inverse(mats, tiles, columns, rows, window):
     count, n, _ = mats.shape
     each = range(count)
+    tiles, saved = tiles[:count], tiles[count:]
     last = n // TILE - 1
 
-    def begin(k):
+    def begin(k, m):
         at = pl.multiple_of(k * TILE, TILE)
         here = pl.ds(at, TILE)
         row = lax.broadcasted_iota(jnp.int32, (n, TILE), 0)
         pivot_rows = (row >= at) & (row < at + TILE)
-        for m in each:
-            inverse = tiles[m][...]
-            scaled = dot3(inverse, mats[m, here, :])
-            columns[m] = left(jnp.where(pivot_rows, 0.0, mats[m, :, here]))
-            mats[m, :, here] = jnp.zeros((n, TILE), F32)
-            mats[m, here, :] = scaled
-            mats[m, here, here] = inverse
-            rows[m] = right(mats[m, here, :])
+        inverse = saved[m][...]
+        scaled = dot3(inverse, mats[m, here, :])
+        columns[m] = left(jnp.where(pivot_rows, 0.0, mats[m, :, here]))
+        mats[m, :, here] = jnp.zeros((n, TILE), F32)
+        mats[m, here, :] = scaled
+        mats[m, here, here] = inverse
+        rows[m] = right(mats[m, here, :])
 
     def update(m, c):
         at = slice(c, c + CHUNK)
@@ -157,18 +157,24 @@
     work = [functools.partial(update, m, c) for c in range(0, n, CHUNK) for m in each]
 
     def step(k, carry):
-        begin(k)
+        here = pl.ds(pl.multiple_of(k * TILE, TILE), TILE)
         after = pl.ds(pl.multiple_of((k + 1) * TILE, TILE), TILE)
         for m in each:
-            tiles[m][...] = mats[m, after, after] - mm(columns[m, after, :], rows[m, :, after])
-        invert_tiles([tiles[m] for m in each], reach, work)
+            inverse = tiles[m][...]
+            saved[m][...] = inverse
+            scaled = dot3(inverse, mats[m, here, after])
+            tiles[m][...] = mats[m, after, after] - dot3(mats[m, after, here], scaled)
+        begins = [functools.partial(begin, k, m) for m in each]
+        invert_tiles([tiles[m] for m in each], window, begins + work)
         return carry
 
     for m in each:
         tiles[m][...] = mats[m, :TILE, :TILE]
-    invert_tiles([tiles[m] for m in each], reach)
+    invert_tiles([tiles[m] for m in each], window)
     lax.fori_loop(0, last, step, 0)
-    begin(last)
+    for m in each:
+        saved[m][...] = tiles[m][...]
+        begin(last, m)
     for item in work:
         item()
 
@@ -236,7 +242,7 @@
             block = inverses[m, down, down]
             extra = jnp.where(eye, diag[m][:, down], 0.0)
             inverses[m, down, down] = 0.5 * (block + block.T) + extra
-    sweep_inverse(inverses, tiles, columns, rows, 64)
+    sweep_inverse(inverses, tiles, columns, rows, 32)
     store = pltpu.make_async_copy(inverses, inverses_hbm, sems.at[2])
     store.start()
     own_state = [state[s : s + 1, :] for s in range(3)]
@@ -324,11 +330,11 @@
             block = get(row, TILE)
             row += TILE
             if i == j:
-                block = block + jnp.where(eye, first_diag[:, i : i + TILE], 0.0)
+                block = block + jnp.where(eye, first_diag[i : i + TILE].reshape(1, TILE), 0.0)
             schur[i : i + TILE, j : j + TILE] = block
     tail = get(row, 8)
     gradient = jnp.concatenate([tail[t : t + 1, :] for t in range(count)], axis=1)
-    rhs[...] = as_column(gradient - first_rhs[...])
+    rhs[...] = as_column(gradient - first_rhs[...].reshape(1, nb))
 
     def eliminate(k):
         here, below = slice(k * TILE, (k + 1) * TILE), slice((k + 1) * TILE, nb)
@@ -354,7 +360,7 @@
             pl.when(k == done)(functools.partial(eliminate, done - 1))
         here = pl.ds(pl.multiple_of(k * TILE, TILE), TILE)
         tile[...] = schur[here, here]
-        invert_tiles([tile], TILE)
+        invert_tiles([tile], TILE // 2)
         return carry
 
     lax.fori_loop(0, count, step, 0)
@@ -365,7 +371,7 @@
         x = heads[k : k + 1, :] - jnp.sum(found_column * below, axis=0, keepdims=True)
         found_row = jnp.concatenate([x, found_row], axis=1)
         found_column = jnp.concatenate([as_column(x), found_column], axis=0)
-    first_step[...] = found_row
+    first_step[...] = found_row.reshape(nb)
     for load in loads:
         load.wait()
     v = jnp.sum(border[...] * found_row, axis=1, keepdims=True)
@@ -405,7 +411,7 @@
         pltpu.VMEM((count, n, 3 * TILE), BF16),
         pltpu.VMEM((count, 3 * TILE, n), BF16),
         pltpu.SemaphoreType.DMA((3,)),
-        *(pltpu.VMEM((TILE, TILE), F32) for _ in range(count)),
+        *(pltpu.VMEM((TILE, TILE), F32) for _ in range(2 * count)),
     ]
 
 
@@ -482,7 +488,7 @@
     first_step, steps, sent = pl.pallas_call(
         finish_kernel,
         out_shape=(
-            jax.ShapeDtypeStruct((1, nb), F32),
+            jax.ShapeDtypeStruct((nb,), F32),
             jax.ShapeDtypeStruct((HOURS, nb), F32),
             jax.ShapeDtypeStruct((1, nb), F32),
         ),
@@ -493,14 +499,14 @@
         ],
         compiler_params=PARAMS,
         name="finish",
-    )(place, mine, other, first_diag[None], first_rhs[None], avail, solved, border, inverses)
+    )(place, mine, other, first_diag, first_rhs, avail, solved, border, inverses)
     returned = lax.ppermute(sent, CORE, pair)
     slot = jnp.arange(3, dtype=jnp.int32)[:, None]
     lead = jnp.where(second & three, returned, jnp.where(second & ~two, steps[1:], steps[:1]))
     middle = jnp.where(second & three, steps[:1], steps[1:])
     end = jnp.where(second, steps[1:], returned)
     chosen = jnp.where(slot == 0, lead, jnp.where(slot == 1, middle, end))
-    return jnp.where(slot < count, chosen, 0.0), first_step[0]
+    return jnp.where(slot < count, chosen, 0.0), first_step
 
 
 def solution(mesh):

time: 154 us -> 152 us (0.987)
  waiting for transfers between devices: 3.22 us -> 5.42 us
  Pallas kernels: 86.1 us -> 84.2 us
    pallas_call x1, Pallas kernels: 54.6 us -> 49.9 us  [on_device(): pl.pallas_call(hours_kernel, out_shape=(jax.ShapeDtypeStruct((HOURS, nb,...]
    pallas_call x1, Pallas kernels: 29.2 us -> 32 us  [on_device(): pl.pallas_call(finish_kernel, out_shape=(jax.ShapeDtypeStruct((nb,), F32)...]
    unnamed x13 -> x9, local copies, waits for them, and re-layouts: 4.62 us -> 4.59 us
  transfers between devices with their start and end apart: 5 -> 5, of which waited for: 2 -> 3; matrix products, arithmetic and copies ran while one was open for 4% -> 2% of each run, Pallas kernels for 0% -> 0%
where the time goes in v4:
time: 152 us; the launch traced here: 151 us
  Pallas kernels  84.2 us (55%)
  blocking collectives  44.1 us (29%)
  starting transfers between devices  8.25 us (5%)
  waiting for transfers between devices  5.42 us (4%)
  local copies, waits for them, and re-layouts  4.65 us (3%)
  other arithmetic  3.36 us (2%)
    pallas_call x1, Pallas kernels, on_device(): pl.pallas_call(hours_kernel, out_shape=(jax.ShapeDtypeStruct((HOURS, nb,...  49.9 us
    pallas_call x1, Pallas kernels, on_device(): pl.pallas_call(finish_kernel, out_shape=(jax.ShapeDtypeStruct((nb,), F32)...  32 us
    all_to_all x1, blocking collectives, summed_over_chips(): piece = lax.all_to_all(pieces, CHIPS, 0, 0, tiled=True).sum(axis=0)  25.8 us
    all_to_all x1, blocking collectives, summed_over_chips(): return lax.all_to_all(spread, CHIPS, 0, 0, tiled=True).reshape(rows, width)  18.3 us
    unnamed x9, local copies, waits for them, and re-layouts  4.59 us
    ppermute x1, starting transfers between devices, on_device(): lax.ppermute(last, GRP_BLK, [(d, d + 1) for d in range(devices - 1)])  3.19 us
    ppermute x1, starting transfers between devices, on_device(): other = lax.ppermute(mine, CORE, pair)  3.13 us
  transfers between devices with their start and end apart: 5, of which 3 were waited for; matrix products, arithmetic and copies ran while one was open for 2% of the time, Pallas kernels for 0%

profile of v4, /device:TPU:1, one launch (start us, length us, event | category | flops | bytes accessed | tf_op | source)
XLA Modules:
  0.0 151.3 jit_solution(9089200073243648098)
XLA Ops:
  1.3 0.6 pad_add_fusion.place
  1.9 2.3 %message.1 = (f32[3,128]{1,0:T(4,128)}, f32[1,128]{1,0:T(1,128)}, f32[1,4096]{1,0:T(1,128)}) custom-call(s32[2]{0:T(128)} %pad_add_fusion.place, f32[3,1536]{1,0:T(4,128)} %barrier_scale.3, f32[3,768]{1,0:T(4,128)} %regularizer.3, f32[3,768]{1,0:T(4,128)} %availability.3, f32[3,768]{1,0:T(4,128)} %block_rhs.3, s32[3,128]{1,0:T(4,128)} %link_mask.3, ...), custom_call_target="tpu_custom_call" | custom-call | tf_op jit(solution)/shard_map/message/pallas_call | solution.py:449
  4.1 1.4 collective-permute-start.1
  5.5 3.2 %collective-permute-start = (f32[1,128]{1,0:T(1,128)}, f32[1,128]{1,0:T(1,128)S(1)}, u32[]{:S(2)}, u32[]{:S(2)}) collective-permute-start(f32[1,128]{1,0:T(1,128)} %get-tuple-element.14), channel_id=1, source_target_pairs={{0,1},{1,2},{2,3},{3,4},{4,5},{5,6},{6,7},{7,8},{8,9},{9,10},{10,1... | collective-permute-start | bytes 1544 | tf_op jit(solution)/shard_map/ppermute | solution.py:460
  8.7 3.1 %copy.15 = f32[768,768]{0,1:T(8,128)} copy(f32[768,768]{1,0:T(8,128)} %border_hbm.3) | data formatting | bytes 4718592 | tf_op args[8]
  11.8 0.0 collective-permute-done.incoming
  11.8 0.0 copy-start.3
  11.8 0.0 collective-permute-done.1.message
  11.8 0.0 copy-start.2
  11.8 0.5 copy-done.3
  12.3 0.1 copy-done.2
  12.4 49.9 %hours.1 = (f32[2,768,768]{2,1,0:T(8,128)}, f32[1536,128]{1,0:T(8,128)}, f32[1536,128]{1,0:T(8,128)}, f32[2,768]{1,0:T(2,128)}, f32[2,768]{1,0:T(2,128)}) custom-call(s32[2]{0:T(128)} %pad_add_fusion.place, f32[3,1536]{1,0:T(4,128)} %barrier_scale.3, f32[3,768]{1,0:T(4,128)} %regularizer.3, f32[3,768]{1,0:T(4,128)} %availability.3, f32[3,768]{1,0:T(4,128)} %block_rhs.3, ...), custom_call_target="tpu_custom_call" | custom-call | tf_op jit(solution)/shard_map/hours/pallas_call | solution.py:466
  62.3 0.1 collective-permute-start.2
  62.4 2.5 %collective-permute-done.2 = f32[1536,128]{1,0:T(8,128)S(1)} collective-permute-done((f32[1536,128]{1,0:T(8,128)}, f32[1536,128]{1,0:T(8,128)S(1)}, u32[]{:S(2)}, u32[]{:S(2)}) %collective-permute-start.2) | collective-permute-done | bytes 786464 | tf_op jit(solution)/shard_map/ppermute | solution.py:486
  64.9 1.2 add.3
  66.1 25.8 %all_to_all.10 = f32[64,24,128]{2,1,0:T(8,128)S(1)} all-to-all(f32[64,24,128]{2,1,0:T(8,128)S(1)} %bitcast.9), channel_id=1, replica_groups=mesh['grp'=4,'blk_0'=4,'blk_1'=4,'blk_2'=2] {'grp','blk_0','blk_1'}, dimensions={0} | all-to-all | bytes 1572864 | tf_op jit(solution)/shard_map/all_to_all | solution.py:431
  91.9 0.1 reduce_sum.9
  92.0 0.1 broadcast_in_dim.67
  92.1 18.3 %all_to_all.11 = f32[64,24,128]{2,1,0:T(8,128)S(1)} all-to-all(f32[64,24,128]{2,1,0:T(8,128)S(1)} %broadcast_in_dim.67), channel_id=1, replica_groups=mesh['grp'=4,'blk_0'=4,'blk_1'=4,'blk_2'=2] {'grp','blk_0','blk_1'}, dimensions={0} | all-to-all | bytes 1572864 | tf_op jit(solution)/shard_map/all_to_all | solution.py:433
  110.3 0.0 copy-start
  110.3 3.1 %collective-permute-start.3 = (f32[1536,128]{1,0:T(8,128)S(1)}, f32[1536,128]{1,0:T(8,128)S(1)}, u32[]{:S(2)}, u32[]{:S(2)}) collective-permute-start(f32[1536,128]{1,0:T(8,128)S(1)} %bitcast.10), channel_id=1, source_target_pairs={{0,1},{1,0},{2,3},{3,2},{4,5},{5,4},{6,7},{7,6},{8,9},{9,8},{10,11... | collective-permute-start | bytes 2359304 | tf_op jit(solution)/shard_map/ppermute | solution.py:487
  113.5 1.9 %collective-permute-done.3.other = f32[1536,128]{1,0:T(8,128)S(1)} collective-permute-done((f32[1536,128]{1,0:T(8,128)S(1)}, f32[1536,128]{1,0:T(8,128)S(1)}, u32[]{:S(2)}, u32[]{:S(2)}) %collective-permute-start.3) | collective-permute-done | bytes 786464 | tf_op jit(solution)/shard_map/ppermute | solution.py:487
  115.4 0.0 copy-start.1
  115.4 0.0 copy-done
  115.4 0.9 copy-done.1
  116.3 32.0 %finish.1 = (f32[768]{0:T(1024)}, f32[2,768]{1,0:T(2,128)}, f32[1,768]{1,0:T(1,128)}) custom-call(s32[2]{0:T(128)} %pad_add_fusion.place, f32[1536,128]{1,0:T(8,128)} %bitcast.11, f32[1536,128]{1,0:T(8,128)} %copy-done.1, f32[768]{0:T(1024)} %first_diag.1, f32[768]{0:T(1024)} %first_rhs.1, f32[2,768]{1,0:T(2,128)} %get-tuple-element.18.avail, ...), custom_call_target="tpu_custom_call" | custom-call | tf_op jit(solution)/shard_map/finish/pallas_call | solution.py:488
  148.4 0.5 collective-permute-start.4
  148.8 1.0 collective-permute-done.4
  149.9 0.8 fusion
  150.7 0.7 select_select_fusion
  (2 shorter events, 0.0 us)
Async XLA Ops:
  4.1 7.7 %collective-permute-start.1 = (f32[1,4096]{1,0:T(1,128)}, f32[1,4096]{1,0:T(1,128)S(1)}, u32[]{:S(2)}, u32[]{:S(2)}) collective-permute-start(f32[1,4096]{1,0:T(1,128)} %get-tuple-element.15), channel_id=1, source_target_pairs={{0,1},{1,0},{2,3},{3,2},{4,5},{5,4},{6,7},{7,6},{8,9},{9,8},{10,11... | collective-permute-start | bytes 49160 | tf_op jit(solution)/shard_map/ppermute | solution.py:461
  5.5 6.3 %collective-permute-start = (f32[1,128]{1,0:T(1,128)}, f32[1,128]{1,0:T(1,128)S(1)}, u32[]{:S(2)}, u32[]{:S(2)}) collective-permute-start(f32[1,128]{1,0:T(1,128)} %get-tuple-element.14), channel_id=1, source_target_pairs={{0,1},{1,2},{2,3},{3,4},{4,5},{5,6},{6,7},{7,8},{8,9},{9,10},{10,1... | collective-permute-start | bytes 1544 | tf_op jit(solution)/shard_map/ppermute | solution.py:460
  11.8 0.5 copy-start.3
  11.8 0.6 copy-start.2
  62.3 2.6 %collective-permute-start.2 = (f32[1536,128]{1,0:T(8,128)}, f32[1536,128]{1,0:T(8,128)S(1)}, u32[]{:S(2)}, u32[]{:S(2)}) collective-permute-start(f32[1536,128]{1,0:T(8,128)} %get-tuple-element.17), channel_id=1, source_target_pairs={{0,1},{1,0},{2,3},{3,2},{4,5},{5,4},{6,7},{7,6},{8,9},{9,8},{10,11... | collective-permute-start | bytes 2359304 | tf_op jit(solution)/shard_map/ppermute | solution.py:486
  110.3 5.1 %copy-start = (f32[64,24,128]{2,1,0:T(8,128)}, f32[64,24,128]{2,1,0:T(8,128)S(1)}, u32[]{:S(2)}) copy-start(f32[64,24,128]{2,1,0:T(8,128)S(1)} %all_to_all.11) | copy-start | bytes 2359300
  110.3 5.0 %collective-permute-start.3 = (f32[1536,128]{1,0:T(8,128)S(1)}, f32[1536,128]{1,0:T(8,128)S(1)}, u32[]{:S(2)}, u32[]{:S(2)}) collective-permute-start(f32[1536,128]{1,0:T(8,128)S(1)} %bitcast.10), channel_id=1, source_target_pairs={{0,1},{1,0},{2,3},{3,2},{4,5},{5,4},{6,7},{7,6},{8,9},{9,8},{10,11... | collective-permute-start | bytes 2359304 | tf_op jit(solution)/shard_map/ppermute | solution.py:487
  115.4 0.9 copy-start.1
  148.4 1.5 collective-permute-start.4

commit v5 on v4

--- a/solution.py
+++ b/solution.py
@@ -242,7 +242,7 @@
             block = inverses[m, down, down]
             extra = jnp.where(eye, diag[m][:, down], 0.0)
             inverses[m, down, down] = 0.5 * (block + block.T) + extra
-    sweep_inverse(inverses, tiles, columns, rows, 32)
+    sweep_inverse(inverses, tiles, columns, rows, PANEL)
     store = pltpu.make_async_copy(inverses, inverses_hbm, sems.at[2])
     store.start()
     own_state = [state[s : s + 1, :] for s in range(3)]
@@ -306,7 +306,7 @@
 
 def finish_kernel(
     place, mine, other, first_diag, first_rhs, avail, solved, border_hbm, inverses_hbm,
-    first_step, steps, sent,
+    first_step, slots, sent,
     schur, rhs, heads, border, inverses, sems, tile,
 ):
     nb = schur.shape[0]
@@ -360,7 +360,7 @@
             pl.when(k == done)(functools.partial(eliminate, done - 1))
         here = pl.ds(pl.multiple_of(k * TILE, TILE), TILE)
         tile[...] = schur[here, here]
-        invert_tiles([tile], TILE // 2)
+        invert_tiles([tile], TILE)
         return carry
 
     lax.fori_loop(0, count, step, 0)
@@ -375,12 +375,20 @@
     for load in loads:
         load.wait()
     v = jnp.sum(border[...] * found_row, axis=1, keepdims=True)
+    steps = []
     for m in range(HOURS):
         w = as_column(avail[m : m + 1, :]) * v
-        steps[m : m + 1, :] = solved[m : m + 1, :] - jnp.sum(
-            w * inverses[m], axis=0, keepdims=True
+        steps.append(
+            solved[m : m + 1, :] - jnp.sum(w * inverses[m], axis=0, keepdims=True)
         )
-    sent[...] = jnp.where(place[1] == 1, steps[0:1, :], steps[1:2, :])
+    early, late = steps
+    zero = jnp.zeros_like(early)
+    held, second = place[0], place[1] == 1
+    two, three = held >= 2, held == 3
+    sent[...] = jnp.where(second, early, late)
+    slots[0:1, :] = jnp.where(second & jnp.logical_not(two), late, early)
+    slots[1:2, :] = jnp.where(two, jnp.where(second & three, early, late), zero)
+    slots[2:3, :] = jnp.where(second & three, late, zero)
 
 
 def message_kernel(
@@ -440,11 +448,9 @@
     nb, nv = constraints.shape
     count = counts[0]
     core = lax.axis_index(CORE)
-    second = core == 1
     devices = lax.axis_size(GRP_BLK)
     pair = [(0, 1), (1, 0)]
     place = jnp.stack([count, core])
-    three, two = count == 3, count >= 2
     nk = link_in.shape[1]
     state, last, lent = pl.pallas_call(
         message_kernel,
@@ -485,11 +491,11 @@
     )
     mine = summed_over_chips(kept + lax.ppermute(sent, CORE, pair))
     other = lax.ppermute(mine, CORE, pair)
-    first_step, steps, sent = pl.pallas_call(
+    first_step, slots, sent = pl.pallas_call(
         finish_kernel,
         out_shape=(
             jax.ShapeDtypeStruct((nb,), F32),
-            jax.ShapeDtypeStruct((HOURS, nb), F32),
+            jax.ShapeDtypeStruct((3, nb), F32),
             jax.ShapeDtypeStruct((1, nb), F32),
         ),
         in_specs=spaces(9, (0,), (7, 8)),
@@ -502,11 +508,8 @@
     )(place, mine, other, first_diag, first_rhs, avail, solved, border, inverses)
     returned = lax.ppermute(sent, CORE, pair)
     slot = jnp.arange(3, dtype=jnp.int32)[:, None]
-    lead = jnp.where(second & three, returned, jnp.where(second & ~two, steps[1:], steps[:1]))
-    middle = jnp.where(second & three, steps[:1], steps[1:])
-    end = jnp.where(second, steps[1:], returned)
-    chosen = jnp.where(slot == 0, lead, jnp.where(slot == 1, middle, end))
-    return jnp.where(slot < count, chosen, 0.0), first_step
+    borrowed_slot = jnp.where(count == 3, 2 - 2 * core, -1)
+    return jnp.where(slot == borrowed_slot, returned, slots), first_step
 
 
 def solution(mesh):

time: 152 us -> 146 us (0.961)
  Pallas kernels: 84.2 us -> 78.8 us
    pallas_call x1, Pallas kernels: 49.9 us -> 47.1 us  [on_device(): pl.pallas_call(hours_kernel, out_shape=(jax.ShapeDtypeStruct((HOURS, nb,...]
    pallas_call x1, Pallas kernels: 32 us -> 29.5 us  [on_device(): pl.pallas_call(finish_kernel, out_shape=(jax.ShapeDtypeStruct((nb,), F32)...]
where the time goes in v5:
time: 146 us
  Pallas kernels  78.8 us (54%)
  blocking collectives  44.1 us (30%)
  starting transfers between devices  8.24 us (6%)
  waiting for transfers between devices  5.43 us (4%)
  local copies, waits for them, and re-layouts  4.62 us (3%)
  other arithmetic  3.34 us (2%)
    pallas_call x1, Pallas kernels, on_device(): pl.pallas_call(hours_kernel, out_shape=(jax.ShapeDtypeStruct((HOURS, nb,...  47.1 us
    pallas_call x1, Pallas kernels, on_device(): pl.pallas_call(finish_kernel, out_shape=(jax.ShapeDtypeStruct((nb,), F32)...  29.5 us
    all_to_all x1, blocking collectives, summed_over_chips(): piece = lax.all_to_all(pieces, CHIPS, 0, 0, tiled=True).sum(axis=0)  25.8 us
    all_to_all x1, blocking collectives, summed_over_chips(): return lax.all_to_all(spread, CHIPS, 0, 0, tiled=True).reshape(rows, width)  18.3 us
    unnamed x9, local copies, waits for them, and re-layouts  4.56 us
    ppermute x1, starting transfers between devices, on_device(): lax.ppermute(last, GRP_BLK, [(d, d + 1) for d in range(devices - 1)])  3.19 us
    ppermute x1, starting transfers between devices, on_device(): other = lax.ppermute(mine, CORE, pair)  3.13 us
  transfers between devices with their start and end apart: 5, of which 3 were waited for; matrix products, arithmetic and copies ran while one was open for 2% of the time, Pallas kernels for 0%

profile of v5, /device:TPU:1, one launch (start us, length us, event | category | flops | bytes accessed | tf_op | source)
XLA Modules:
  0.0 145.9 jit_solution(15714287622614292960)
XLA Ops:
  1.3 0.6 pad_add_fusion.place
  1.9 2.3 %message.1 = (f32[3,128]{1,0:T(4,128)}, f32[1,128]{1,0:T(1,128)}, f32[1,4096]{1,0:T(1,128)}) custom-call(s32[2]{0:T(128)} %pad_add_fusion.place, f32[3,1536]{1,0:T(4,128)} %barrier_scale.3, f32[3,768]{1,0:T(4,128)} %regularizer.3, f32[3,768]{1,0:T(4,128)} %availability.3, f32[3,768]{1,0:T(4,128)} %block_rhs.3, s32[3,128]{1,0:T(4,128)} %link_mask.3, ...), custom_call_target="tpu_custom_call" | custom-call | tf_op jit(solution)/shard_map/message/pallas_call | solution.py:455
  4.2 1.4 collective-permute-start.1
  5.6 3.2 %collective-permute-start = (f32[1,128]{1,0:T(1,128)}, f32[1,128]{1,0:T(1,128)S(1)}, u32[]{:S(2)}, u32[]{:S(2)}) collective-permute-start(f32[1,128]{1,0:T(1,128)} %get-tuple-element.14), channel_id=1, source_target_pairs={{0,1},{1,2},{2,3},{3,4},{4,5},{5,6},{6,7},{7,8},{8,9},{9,10},{10,1... | collective-permute-start | bytes 1544 | tf_op jit(solution)/shard_map/ppermute | solution.py:466
  8.8 3.1 %copy.15 = f32[768,768]{0,1:T(8,128)} copy(f32[768,768]{1,0:T(8,128)} %border_hbm.3) | data formatting | bytes 4718592 | tf_op args[8]
  11.9 0.0 collective-permute-done.incoming
  11.9 0.0 copy-start.3
  11.9 0.0 collective-permute-done.1.message
  11.9 0.0 copy-start.2
  11.9 0.6 copy-done.3
  12.5 0.0 copy-done.2
  12.5 47.1 %hours.1 = (f32[2,768,768]{2,1,0:T(8,128)}, f32[1536,128]{1,0:T(8,128)}, f32[1536,128]{1,0:T(8,128)}, f32[2,768]{1,0:T(2,128)}, f32[2,768]{1,0:T(2,128)}) custom-call(s32[2]{0:T(128)} %pad_add_fusion.place, f32[3,1536]{1,0:T(4,128)} %barrier_scale.3, f32[3,768]{1,0:T(4,128)} %regularizer.3, f32[3,768]{1,0:T(4,128)} %availability.3, f32[3,768]{1,0:T(4,128)} %block_rhs.3, ...), custom_call_target="tpu_custom_call" | custom-call | tf_op jit(solution)/shard_map/hours/pallas_call | solution.py:472
  59.6 0.1 collective-permute-start.2
  59.6 2.5 %collective-permute-done.2 = f32[1536,128]{1,0:T(8,128)S(1)} collective-permute-done((f32[1536,128]{1,0:T(8,128)}, f32[1536,128]{1,0:T(8,128)S(1)}, u32[]{:S(2)}, u32[]{:S(2)}) %collective-permute-start.2) | collective-permute-done | bytes 786464 | tf_op jit(solution)/shard_map/ppermute | solution.py:492
  62.1 1.2 add.3
  63.4 25.8 %all_to_all.10 = f32[64,24,128]{2,1,0:T(8,128)S(1)} all-to-all(f32[64,24,128]{2,1,0:T(8,128)S(1)} %bitcast.6), channel_id=1, replica_groups=mesh['grp'=4,'blk_0'=4,'blk_1'=4,'blk_2'=2] {'grp','blk_0','blk_1'}, dimensions={0} | all-to-all | bytes 1572864 | tf_op jit(solution)/shard_map/all_to_all | solution.py:439
  89.2 0.1 reduce_sum.9
  89.2 0.1 broadcast_in_dim.26
  89.3 18.3 %all_to_all.11 = f32[64,24,128]{2,1,0:T(8,128)S(1)} all-to-all(f32[64,24,128]{2,1,0:T(8,128)S(1)} %broadcast_in_dim.26), channel_id=1, replica_groups=mesh['grp'=4,'blk_0'=4,'blk_1'=4,'blk_2'=2] {'grp','blk_0','blk_1'}, dimensions={0} | all-to-all | bytes 1572864 | tf_op jit(solution)/shard_map/all_to_all | solution.py:441
  107.6 0.0 copy-start
  107.6 3.1 %collective-permute-start.3 = (f32[1536,128]{1,0:T(8,128)S(1)}, f32[1536,128]{1,0:T(8,128)S(1)}, u32[]{:S(2)}, u32[]{:S(2)}) collective-permute-start(f32[1536,128]{1,0:T(8,128)S(1)} %bitcast.7), channel_id=1, source_target_pairs={{0,1},{1,0},{2,3},{3,2},{4,5},{5,4},{6,7},{7,6},{8,9},{9,8},{10,11... | collective-permute-start | bytes 2359304 | tf_op jit(solution)/shard_map/ppermute | solution.py:493
  110.7 1.9 %collective-permute-done.3.other = f32[1536,128]{1,0:T(8,128)S(1)} collective-permute-done((f32[1536,128]{1,0:T(8,128)S(1)}, f32[1536,128]{1,0:T(8,128)S(1)}, u32[]{:S(2)}, u32[]{:S(2)}) %collective-permute-start.3) | collective-permute-done | bytes 786464 | tf_op jit(solution)/shard_map/ppermute | solution.py:493
  112.6 0.0 copy-start.1
  112.6 0.0 copy-done
  112.6 0.9 copy-done.1
  113.5 29.5 %finish.1 = (f32[768]{0:T(1024)}, f32[3,768]{1,0:T(4,128)}, f32[1,768]{1,0:T(1,128)}) custom-call(s32[2]{0:T(128)} %pad_add_fusion.place, f32[1536,128]{1,0:T(8,128)} %bitcast.8, f32[1536,128]{1,0:T(8,128)} %copy-done.1, f32[768]{0:T(1024)} %first_diag.1, f32[768]{0:T(1024)} %first_rhs.1, f32[2,768]{1,0:T(2,128)} %get-tuple-element.18.avail, ...), custom_call_target="tpu_custom_call" | custom-call | tf_op jit(solution)/shard_map/finish/pallas_call | solution.py:494
  143.0 0.5 collective-permute-start.4
  143.4 1.0 collective-permute-done.4
  144.5 1.4 broadcast_select_fusion
  (2 shorter events, 0.0 us)
Async XLA Ops:
  4.2 7.7 %collective-permute-start.1 = (f32[1,4096]{1,0:T(1,128)}, f32[1,4096]{1,0:T(1,128)S(1)}, u32[]{:S(2)}, u32[]{:S(2)}) collective-permute-start(f32[1,4096]{1,0:T(1,128)} %get-tuple-element.15), channel_id=1, source_target_pairs={{0,1},{1,0},{2,3},{3,2},{4,5},{5,4},{6,7},{7,6},{8,9},{9,8},{10,11... | collective-permute-start | bytes 49160 | tf_op jit(solution)/shard_map/ppermute | solution.py:467
  5.6 6.3 %collective-permute-start = (f32[1,128]{1,0:T(1,128)}, f32[1,128]{1,0:T(1,128)S(1)}, u32[]{:S(2)}, u32[]{:S(2)}) collective-permute-start(f32[1,128]{1,0:T(1,128)} %get-tuple-element.14), channel_id=1, source_target_pairs={{0,1},{1,2},{2,3},{3,4},{4,5},{5,6},{6,7},{7,8},{8,9},{9,10},{10,1... | collective-permute-start | bytes 1544 | tf_op jit(solution)/shard_map/ppermute | solution.py:466
  11.9 0.6 copy-start.3
  11.9 0.6 copy-start.2
  59.6 2.6 %collective-permute-start.2 = (f32[1536,128]{1,0:T(8,128)}, f32[1536,128]{1,0:T(8,128)S(1)}, u32[]{:S(2)}, u32[]{:S(2)}) collective-permute-start(f32[1536,128]{1,0:T(8,128)} %get-tuple-element.17), channel_id=1, source_target_pairs={{0,1},{1,0},{2,3},{3,2},{4,5},{5,4},{6,7},{7,6},{8,9},{9,8},{10,11... | collective-permute-start | bytes 2359304 | tf_op jit(solution)/shard_map/ppermute | solution.py:492
  107.6 5.1 %copy-start = (f32[64,24,128]{2,1,0:T(8,128)}, f32[64,24,128]{2,1,0:T(8,128)S(1)}, u32[]{:S(2)}) copy-start(f32[64,24,128]{2,1,0:T(8,128)S(1)} %all_to_all.11) | copy-start | bytes 2359300
  107.6 5.0 %collective-permute-start.3 = (f32[1536,128]{1,0:T(8,128)S(1)}, f32[1536,128]{1,0:T(8,128)S(1)}, u32[]{:S(2)}, u32[]{:S(2)}) collective-permute-start(f32[1536,128]{1,0:T(8,128)S(1)} %bitcast.7), channel_id=1, source_target_pairs={{0,1},{1,0},{2,3},{3,2},{4,5},{5,4},{6,7},{7,6},{8,9},{9,8},{10,11... | collective-permute-start | bytes 2359304 | tf_op jit(solution)/shard_map/ppermute | solution.py:493
  112.6 0.9 copy-start.1
  143.0 1.5 %collective-permute-start.4 = (f32[1,768]{1,0:T(1,128)}, f32[1,768]{1,0:T(1,128)S(1)}, u32[]{:S(2)}, u32[]{:S(2)}) collective-permute-start(f32[1,768]{1,0:T(1,128)} %get-tuple-element.21), channel_id=1, source_target_pairs={{0,1},{1,0},{2,3},{3,2},{4,5},{5,4},{6,7},{7,6},{8,9},{9,8},{10,11... | collective-permute-start | bytes 9224 | tf_op jit(solution)/shard_map/ppermute | solution.py:509
